TPU v7x, 512 devices: a whole 4x4x16 slice. The times are simulated.
512 devices in a mesh: hot: 32 (over z_hi, x, core), load: 16 (over z_lo, y).
Axes of the slice: x: 4, y: 4, z: 16 (z_hi: 4, z_lo: 4; z = z_hi * 4 + z_lo), core: 2. Of those that a mesh axis runs over, the one named last changes fastest.
Arguments:
- response: bfloat16 [2048, 2048, 128], P('hot', 'load'), may hold values from -1 to 1, as said below
- forces: bfloat16 [2048, 1408], P('load'), may hold values from -6 to 6
- measured: float32 [2048, 384], P('hot'), may hold values from -6 to 6
Outputs:
- updated_forces: float32 [2048, 1408], P('load')
- updated_residual: float32 [2048, 384], P('hot')
Inputs may be any that keep to these rules, and one draw needn't show every extreme that they name: impulse-response coefficients.
All inputs are finite; a program needn't handle non-finite values.
Results may differ from a plain program's by a relative error of at most 0.0041.
Values sent between devices are 32-bit elements; how exact they have to be, the bound alone decides.
No kernel may reach another device: no remote copies, remote signals or barrier semaphores. Data moves between devices by JAX's collectives and lax.ppermute only.
A program may use at most 128 MiB of HBM per device.

v0:
```python
import jax
import jax.numpy as jnp
from jax import lax
from jax.sharding import PartitionSpec as P

TAPS = 128
SEG = 48
CASES = 8
HIST = 128
STEPS = 176


def strain_product(response, signal):
    seg_cols = SEG * CASES
    running = jnp.zeros((response.shape[0], seg_cols), jnp.float32)
    tap_span = min(16, TAPS)
    for first_tap in range(0, TAPS, tap_span):
        window = jnp.stack(
            [
                signal[:, (HIST - tap_index) * CASES : (HIST - tap_index) * CASES + seg_cols]
                for tap_index in range(first_tap, first_tap + tap_span)
            ],
            axis=1,
        )
        running = running + jnp.einsum(
            "hlk,lkm->hm",
            response[:, :, first_tap : first_tap + tap_span],
            window,
            preferred_element_type=jnp.float32,
        )
    return running


def load_product(response, strains):
    col_count = STEPS * CASES
    padded = jnp.pad(strains, ((0, 0), (HIST * CASES, TAPS * CASES)))
    running = jnp.zeros((response.shape[1], col_count), jnp.float32)
    tap_span = min(16, TAPS)
    for first_tap in range(0, TAPS, tap_span):
        window = jnp.stack(
            [
                padded[:, tap_index * CASES : tap_index * CASES + col_count]
                for tap_index in range(first_tap, first_tap + tap_span)
            ],
            axis=1,
        )
        running = running + jnp.einsum(
            "hlk,hkm->lm",
            response[:, :, first_tap : first_tap + tap_span],
            window,
            preferred_element_type=jnp.float32,
        )
    return running


def body(response, forces, measured):
    strains = lax.psum(strain_product(response, forces), "load")
    residual = measured - strains
    residual_b = residual.astype(jnp.bfloat16)
    gradient = lax.psum(load_product(response, residual_b), "hot")
    grad_local = jnp.sum(gradient * gradient)
    grad_total = lax.psum(grad_local, "load")
    gradient_b = gradient.astype(jnp.bfloat16)
    image_sum = lax.psum(strain_product(response, gradient_b), "load")
    image_local = jnp.sum(image_sum * image_sum)
    image_total = lax.psum(image_local, "hot")
    step_size = grad_total / image_total
    return (forces.astype(jnp.float32) + step_size * gradient, residual - step_size * image_sum)


def solution(mesh):
    placed = (P("hot", "load", None), P("load", None), P("hot", None))
    return jax.shard_map(
        body,
        mesh=mesh,
        in_specs=placed,
        out_specs=(P("load", None), P("hot", None)),
        check_vma=False,
    )
```

profile of v0, /device:TPU:1, one launch (start us, length us, event | category | flops | bytes accessed | tf_op | source)
XLA Modules:
  0.0 907.2 jit_solution(11067192214569469330)
XLA Ops:
  7.2 1.3 constant_dynamic-update-slice_fusion.111
  8.5 0.9 constant_dynamic-update-slice_fusion.127
  9.4 1.0 constant_dynamic-update-slice_fusion.126
  10.4 1.0 constant_dynamic-update-slice_fusion.125
  11.4 1.0 constant_dynamic-update-slice_fusion.124
  12.4 1.0 constant_dynamic-update-slice_fusion.123
  13.4 1.0 constant_dynamic-update-slice_fusion.122
  14.4 1.0 constant_dynamic-update-slice_fusion.121
  15.4 1.0 constant_dynamic-update-slice_fusion.120
  16.4 1.0 constant_dynamic-update-slice_fusion.119
  17.4 1.0 constant_dynamic-update-slice_fusion.118
  18.4 1.0 constant_dynamic-update-slice_fusion.117
  19.4 1.0 constant_dynamic-update-slice_fusion.116
  20.4 1.0 constant_dynamic-update-slice_fusion.115
  21.5 1.1 copy-done.7
  22.6 0.5 copy-done.9
  23.1 0.5 copy-done.11
  23.5 0.5 copy-done.13
  24.0 0.5 copy-done.15
  24.6 0.4 copy-done.17
  24.9 0.6 copy-done.19
  25.6 0.7 constant_dynamic-update-slice_fusion.114
  26.3 7.5 fusion.153
  33.8 2.0 copy.31
  35.9 2.7 copy.32
  38.5 2.7 copy.33
  41.2 2.7 copy.34
  43.9 2.7 copy.35
  46.5 2.0 copy.36
  48.6 2.0 copy.37
  50.6 1.0 copy.38
  51.6 1.2 constant_dynamic-update-slice_fusion.113
  52.8 1.2 constant_dynamic-update-slice_fusion.112
  54.0 1.9 convolution_bitcast_fusion.15
  56.0 0.4 fusion.15
  57.0 0.5 copy-done.14
  58.5 0.6 copy-done.10
  60.0 2.4 fusion.9
  62.7 158.2 %all-reduce.5.cloned.1.call-done = f32[64,384]{1,0:T(8,128)} async-done(((f32[64,384]{1,0:T(8,128)}), f32[64,384]{1,0:T(8,128)}) %all-reduce.5.cloned.1.call-update) | async-done | bytes 98320 | tf_op jit(solution)/shard_map/psum | solution.py:57
  220.9 0.9 fusion.152
  229.6 1.0 convolution_bitcast_fusion.3
  230.6 1.0 convolution_bitcast_fusion.4
  231.6 1.0 convolution_bitcast_fusion.5
  232.5 1.0 convolution_bitcast_fusion.6
  235.3 1.0 convolution_bitcast_fusion
  236.2 1.0 convolution_bitcast_fusion.1
  237.2 1.0 fusion.3
  238.2 2.1 fusion.7
  240.4 354.4 %all-reduce.7.cloned.1.call-done = f32[128,1408]{0,1:T(8,128)} async-done(((f32[128,1408]{0,1:T(8,128)}), f32[128,1408]{0,1:T(8,128)}) %all-reduce.7.cloned.1.call-update) | async-done | bytes 720912 | tf_op jit(solution)/shard_map/psum | solution.py:60
  594.8 2.1 fusion.154
  600.3 0.6 convolution_bitcast_fusion.23
  600.9 0.6 fusion.23
  601.5 0.6 fusion.22
  602.1 0.6 fusion.21
  602.7 0.6 fusion.20
  603.3 0.6 fusion.19
  603.9 0.6 fusion.18
  604.6 1.2 fusion.17
  606.1 154.2 %all-reduce.9.cloned.1.call-done = f32[64,384]{1,0:T(8,128)} async-done(((f32[64,384]{1,0:T(8,128)}), f32[64,384]{1,0:T(8,128)}) %all-reduce.9.cloned.1.call-update) | async-done | bytes 98320 | tf_op jit(solution)/shard_map/psum | solution.py:64
  760.2 1.5 multiply_reduce_fusion.1
  761.7 34.8 %psum.37 = f32[]{:T(128)} all-reduce(f32[]{:T(128)} %get-tuple-element.15), channel_id=1, replica_groups=mesh['hot'=32,'load'=16] {'load'}, use_global_device_ids=true, to_apply=%region_3.4 | all-reduce | flops 1 | bytes 8 | tf_op jit(solution)/shard_map/psum | solution.py:62
  796.5 100.9 %psum.39 = f32[]{:T(128)} all-reduce(f32[]{:T(128)} %multiply_reduce_fusion.1), channel_id=1, replica_groups=mesh['hot'=32,'load'=16] {'hot'}, use_global_device_ids=true, to_apply=%region_6.7 | all-reduce | flops 1 | bytes 8 | tf_op jit(solution)/shard_map/psum | solution.py:66
  898.9 1.1 copy.22
  900.0 0.7 multiply_subtract_fusion
  (163 shorter events, 15.9 us)
Async XLA Ops:
  7.2 1.4 copy-start
  7.2 213.7 %all-reduce.5.cloned.1.call-start = ((), (), s32[]{:S(2)}) async-start(), calls=%async_computation | async-start | bytes 196608 | tf_op jit(solution)/shard_map/psum | solution.py:57
  19.4 6.9 copy-start.1
  21.4 1.2 copy-start.7
  21.4 1.6 copy-start.9
  21.4 2.1 copy-start.11
  21.4 2.6 copy-start.13
  21.4 3.1 copy-start.15
  21.4 3.5 copy-start.17
  21.5 4.1 copy-start.19
  52.8 3.2 copy-start.6
  54.0 1.9 copy-start.18
  54.0 2.3 copy-start.5
  54.0 2.4 copy-start.16
  56.0 1.1 copy-start.4
  56.0 1.6 copy-start.14
  56.5 1.5 copy-start.3
  56.5 1.6 copy-start.12
  57.6 1.5 copy-start.10
  58.1 1.5 copy-start.8
  60.0 160.9 %copy-start.21 = (f32[64,384]{1,0:T(8,128)S(1)}, f32[64,384]{1,0:T(8,128)}, u32[]{:S(2)}) copy-start(f32[64,384]{1,0:T(8,128)} %param.5) | copy-start | bytes 294916
  62.5 532.4 %all-reduce.7.cloned.1.call-start = ((), (), s32[]{:S(2)}) async-start(), calls=%async_computation.1 | async-start | bytes 1441792 | tf_op jit(solution)/shard_map/psum | solution.py:60
  240.4 519.9 %all-reduce.9.cloned.1.call-start = ((), (), s32[]{:S(2)}) async-start(), calls=%async_computation.2 | async-start | bytes 196608 | tf_op jit(solution)/shard_map/psum | solution.py:64
  604.5 294.3 %copy-start.2 = (f32[128,1408]{0,1:T(8,128)S(1)}, f32[128,1408]{0,1:T(8,128)}, u32[]{:S(2)}) copy-start(f32[128,1408]{0,1:T(8,128)} %all-reduce.7.cloned.1.call-done) | copy-start | bytes 2162692
  898.8 1.2 copy-start.20
Sparse Core Ops, SparseCore 0:
  62.6 158.2 all-reduce.4
  240.5 354.3 all-reduce.6
  605.9 154.2 all-reduce.8
where the time goes:
time: 908 us; the launch traced here: 907 us
  waiting for transfers between devices  667 us (73%)
  blocking collectives  136 us (15%)
  local copies, waits for them, and re-layouts  62.6 us (7%)
  matrix products  20.8 us (2%)
  between operations  15.7 us (2%)
    psum x1, waiting for transfers between devices, body(): gradient = lax.psum(load_product(response, residual_b), 'hot')  354 us
    psum x1, waiting for transfers between devices, body(): strains = lax.psum(strain_product(response, forces), 'load')  158 us
    psum x1, waiting for transfers between devices, body(): image_sum = lax.psum(strain_product(response, gradient_b), 'load')  154 us
    psum x1, blocking collectives, body(): image_total = lax.psum(image_local, 'hot')  101 us
    unnamed x176, local copies, waits for them, and re-layouts  52.5 us
    psum x1, blocking collectives, body(): grad_total = lax.psum(grad_local, 'load')  34.8 us
  transfers between devices with their start and end apart: 3, of which 3 were waited for; matrix products, arithmetic and copies ran while one was open for 0% of the time, Pallas kernels for 0%

commit v1 on v0

v1 whole, which is shorter than its diff:
```python
import jax
import jax.numpy as jnp
from jax import lax
from jax.experimental import pallas as pl
from jax.experimental.pallas import tpu as pltpu
from jax.sharding import Mesh, PartitionSpec as P

TAPS = 128
SEG = 48
CASES = 8
HIST = 128
STEPS = 176
LANES = 128
PHASES = LANES // CASES
SPANS = TAPS // PHASES
SEG_COLS = SEG * CASES
SEG_BLOCKS = SEG_COLS // LANES
COLS = STEPS * CASES
BLOCKS = COLS // LANES
F32 = jnp.float32
BF16 = jnp.bfloat16
VMEM_LIMIT = 40 * 1024 * 1024


def fill_forward_weights(taps_ref, weights):
    hots = taps_ref.shape[1]
    for tap in range(TAPS):
        span, phase = divmod(tap, PHASES)
        weights[span * hots:(span + 1) * hots, phase * LANES:(phase + 1) * LANES] = taps_ref[tap]


def fill_adjoint_weights(taps_ref, weights):
    hots = taps_ref.shape[1]
    for tap in range(TAPS):
        span, phase = divmod(tap, PHASES)
        weights[phase * hots:(phase + 1) * hots, span * LANES:(span + 1) * LANES] = taps_ref[tap]


def forward_product(signal_t, taps_ref, windows, weights):
    hots = taps_ref.shape[1]
    fill_forward_weights(taps_ref, weights)
    rows = COLS - LANES
    for phase in range(PHASES):
        first = LANES - CASES * phase
        windows[:, phase * LANES:(phase + 1) * LANES] = signal_t[first:first + rows, :].astype(BF16)
    parts = [None] * SEG_BLOCKS
    for block in range(1, BLOCKS, 2):
        low = max(SPANS - 1 - block, 0)
        high = min(SPANS + 2 - block, SPANS - 1)
        out = lax.dot_general(
            windows[(block - 1) * LANES:(block + 1) * LANES, :],
            weights[low * hots:(high + 1) * hots, :],
            (((1,), (1,)), ((), ())),
            preferred_element_type=F32,
        )
        for half in range(2):
            for span in range(low, high + 1):
                target = block + half + span - SPANS
                if 0 <= target < SEG_BLOCKS:
                    piece = out[half * LANES:(half + 1) * LANES, (span - low) * hots:(span - low + 1) * hots]
                    parts[target] = piece if parts[target] is None else parts[target] + piece
    return jnp.concatenate(parts, axis=0)


def pack_strains(value, out_ref, scratch):
    half = SEG_COLS // 2
    hots = value.shape[1]
    scratch[:, 0:hots] = value[0:half]
    scratch[:, hots:2 * hots] = value[half:]
    chunks = out_ref.shape[0]
    size = half // chunks
    for chunk in range(chunks):
        out_ref[chunk, 0:size, :] = scratch[chunk * size:(chunk + 1) * size, :]


def unpack_strains(chunks_ref, scratch):
    chunks = chunks_ref.shape[0]
    size = (SEG_COLS // 2) // chunks
    for chunk in range(chunks):
        scratch[chunk * size:(chunk + 1) * size, :] = chunks_ref[chunk, 0:size, :]


def strain_kernel(taps_ref, forces_ref, measured_ref, part_ref, measured_t_ref, signal_t, windows, weights, packed):
    for block in range(BLOCKS):
        cols = slice(block * LANES, (block + 1) * LANES)
        signal_t[cols, :] = forces_ref[:, cols].astype(F32).T
    result = forward_product(signal_t, taps_ref, windows, weights)
    part_ref[...] = jnp.zeros_like(part_ref)
    pack_strains(result, part_ref, packed)
    half = SEG_COLS // 2
    hots = measured_ref.shape[0]
    measured_t = measured_ref[...].T
    measured_t_ref[:, 0:hots] = measured_t[0:half]
    measured_t_ref[:, hots:2 * hots] = measured_t[half:]


def gradient_kernel(taps_ref, strains_ref, measured_t_ref, part_ref, residual_ref, packed, padded, windows, weights, total):
    hots = taps_ref.shape[1]
    half = SEG_COLS // 2
    unpack_strains(strains_ref, packed)
    residual = measured_t_ref[...] - packed[...]
    residual_ref[...] = residual
    padded[...] = jnp.zeros_like(padded)
    for lane, shift in ((0, 0), (hots, CASES)):
        padded[LANES - shift:LANES - shift + half, lane:lane + hots] = residual[:, 0:hots]
        padded[LANES - shift + half:LANES - shift + 2 * half, lane:lane + hots] = residual[:, hots:2 * hots]
    fill_adjoint_weights(taps_ref, weights)
    rows = windows.shape[0]
    for pair in range(PHASES // 2):
        first = 2 * CASES * pair
        windows[:, pair * 2 * hots:(pair + 1) * 2 * hots] = padded[first:first + rows, :].astype(BF16)
    seen = set()
    for span in range(0, SPANS, 2):
        out = jnp.dot(windows[...], weights[:, span * LANES:(span + 2) * LANES], preferred_element_type=F32)
        for side in range(2):
            for row in range(rows // LANES):
                block = row - 1 + SPANS - (span + side)
                piece = out[row * LANES:(row + 1) * LANES, side * LANES:(side + 1) * LANES]
                cols = slice(block * LANES, (block + 1) * LANES)
                if block in seen:
                    total[cols, :] += piece
                else:
                    total[cols, :] = piece
                    seen.add(block)
    chunks = part_ref.shape[0]
    size = COLS // chunks
    for chunk in range(chunks):
        part_ref[chunk, 0:size, :] = total[chunk * size:(chunk + 1) * size, :]
        part_ref[chunk, size:, :] = jnp.zeros((part_ref.shape[1] - size, LANES), F32)


def image_kernel(taps_ref, gradient_ref, part_ref, signal_t, windows, weights, packed):
    chunks = gradient_ref.shape[0]
    size = COLS // chunks
    for chunk in range(chunks):
        signal_t[chunk * size:(chunk + 1) * size, :] = gradient_ref[chunk, 0:size, :]
    result = forward_product(signal_t, taps_ref, windows, weights)
    gradient = signal_t[...]
    squares = jnp.sum(gradient * gradient, axis=0, keepdims=True)
    pack_strains(result, part_ref, packed)
    size = (SEG_COLS // 2) // part_ref.shape[0]
    for chunk in range(part_ref.shape[0]):
        part_ref[chunk, size:, :] = jnp.broadcast_to(squares, (part_ref.shape[1] - size, LANES))


def update_kernel(forces_ref, gradient_ref, image_ref, residual_ref, forces_out, residual_out, signal_t, packed):
    size = (SEG_COLS // 2) // image_ref.shape[0]
    squares = image_ref[0, size:size + 1, :]
    image_squares = jnp.zeros((1, LANES), F32)
    for chunk in range(image_ref.shape[0]):
        image_squares = image_squares + image_ref[chunk, size + 1:size + 2, :]
    step_size = jnp.sum(squares, axis=1, keepdims=True) / jnp.sum(image_squares, axis=1, keepdims=True)
    unpack_strains(image_ref, packed)
    left = residual_ref[...] - step_size * packed[...]
    hots = residual_out.shape[0]
    half = SEG_COLS // 2
    left_t = jnp.concatenate([left[:, 0:hots], left[:, hots:2 * hots]], axis=0)
    residual_out[...] = left_t.T
    chunks = gradient_ref.shape[0]
    size = COLS // chunks
    for chunk in range(chunks):
        signal_t[chunk * size:(chunk + 1) * size, :] = gradient_ref[chunk, 0:size, :]
    for block in range(BLOCKS):
        cols = slice(block * LANES, (block + 1) * LANES)
        forces_out[:, cols] = forces_ref[:, cols].astype(F32) + step_size * signal_t[cols, :].T


def call(kernel, outs, scratch):
    return pl.pallas_call(
        kernel,
        out_shape=outs,
        scratch_shapes=scratch,
        compiler_params=pltpu.CompilerParams(vmem_limit_bytes=VMEM_LIMIT),
    )


def body(response, forces, measured):
    hots, loads, _ = response.shape
    load_axes, near_axes = ("zl", "y"), ("zh", "x")
    peers = lax.axis_size(load_axes)
    near = lax.axis_size(near_axes)
    hot_peers = near * lax.axis_size("c")
    half = SEG_COLS // 2
    chunk_rows = -(-(half // peers + 2) // 8) * 8
    grad_rows = -(-(COLS // hot_peers) // 8) * 8
    part = jax.ShapeDtypeStruct((peers, chunk_rows, LANES), F32)
    packed_shape = jax.ShapeDtypeStruct((half, 2 * hots), F32)
    forward_scratch = [
        pltpu.VMEM((COLS, loads), F32),
        pltpu.VMEM((COLS - LANES, PHASES * loads), BF16),
        pltpu.VMEM((SPANS * hots, PHASES * loads), BF16),
        pltpu.VMEM((half, 2 * hots), F32),
    ]

    def spread(value, count):
        return jnp.broadcast_to(value[None], (count,) + value.shape)

    taps = jnp.transpose(response, (2, 0, 1))
    strain_part, measured_t = call(strain_kernel, (part, packed_shape), forward_scratch)(taps, forces, measured)
    got = lax.all_to_all(strain_part, load_axes, 0, 0)
    strains = lax.all_to_all(spread(jnp.sum(got, axis=0), peers), load_axes, 0, 0)
    grad_part, residual = call(
        gradient_kernel,
        (jax.ShapeDtypeStruct((hot_peers, grad_rows, LANES), F32), packed_shape),
        [
            pltpu.VMEM((half, 2 * hots), F32),
            pltpu.VMEM((SEG_COLS + 2 * LANES, 2 * hots), F32),
            pltpu.VMEM((SEG_COLS + LANES, PHASES * hots), BF16),
            pltpu.VMEM((PHASES * hots, SPANS * loads), BF16),
            pltpu.VMEM((COLS, loads), F32),
        ],
    )(taps, strains, measured_t)
    got = lax.all_to_all(grad_part.reshape(2, near, grad_rows, LANES), "c", 0, 0)
    got = lax.all_to_all(got[0] + got[1], near_axes, 0, 0)
    got = lax.all_to_all(spread(jnp.sum(got, axis=0), near), near_axes, 0, 0)
    gradient = lax.all_to_all(spread(got, 2), "c", 0, 0).reshape(hot_peers, grad_rows, LANES)
    image_part = call(image_kernel, part, forward_scratch)(taps, gradient)
    image = jnp.sum(lax.all_to_all(image_part, load_axes, 0, 0), axis=0)
    rows = half // peers
    squares = jnp.sum(image[:rows] * image[:rows], axis=0, keepdims=True)
    squares = lax.all_to_all(spread(squares, hot_peers), ("zh", "x", "c"), 0, 0)
    squares = jnp.sum(squares, axis=0)
    image = jnp.concatenate([image[:rows + 1], squares, image[rows + 2:]], axis=0)
    image = lax.all_to_all(spread(image, peers), load_axes, 0, 0)
    return call(
        update_kernel,
        (jax.ShapeDtypeStruct((loads, COLS), F32), jax.ShapeDtypeStruct((hots, SEG_COLS), F32)),
        [pltpu.VMEM((COLS, loads), F32), pltpu.VMEM((half, 2 * hots), F32)],
    )(forces, gradient, image, residual)


def solution(mesh):
    parts = Mesh(mesh.devices.reshape(4, 4, 2, 4, 4), ("zh", "x", "c", "zl", "y"))
    hot, load = ("zh", "x", "c"), ("zl", "y")
    return jax.shard_map(
        body,
        mesh=parts,
        in_specs=(P(hot, load, None), P(load, None), P(hot, None)),
        out_specs=(P(load, None), P(hot, None)),
        check_vma=False,
    )
```

time: 908 us -> 166 us (0.18)
  waiting for transfers between devices: 667 us -> 14.1 us
  local copies, waits for them, and re-layouts: 62.6 us -> 4.08 us
  matrix products: 20.8 us -> 0 us
  between operations: 15.7 us -> 0.74 us
    psum x3 -> x0, waiting for transfers between devices: 667 us -> none  [the longest x1 354 us: body(): gradient = lax.psum(load_product(response, residual_b), 'hot')]
    psum x2 -> x0, blocking collectives: 136 us -> none  [the longest x1 101 us: body(): image_total = lax.psum(image_local, 'hot')]
    all_to_all x0 -> x8, blocking collectives: none -> 132 us  [the longest x1 37.7 us: body(): got = lax.all_to_all(got[0] + got[1], near_axes, 0, 0)]
    unnamed x176 -> x5, local copies, waits for them, and re-layouts: 52.5 us -> 3.36 us
    dot_general x24 -> x0, matrix products: 20.8 us -> none  [the longest x16 11.9 us: strain_product(): jnp.einsum('hlk,lkm->hm', response[:, :, first_tap:first_tap + tap_span],...]
    all_to_all x0 -> x1, waiting for transfers between devices: none -> 14.1 us  [body(): squares = lax.all_to_all(spread(squares, hot_peers), ('zh', 'x', 'c'), 0, 0)]
  transfers between devices with their start and end apart: 3 -> 1, of which waited for: 3 -> 1; matrix products, arithmetic and copies ran while one was open for 0% -> 0% of each run, Pallas kernels for 0% -> 0%
where the time goes in v1:
time: 166 us
  blocking collectives  132 us (80%)
  waiting for transfers between devices  14.1 us (8%)
  starting transfers between devices  7.4 us (4%)
  Pallas kernels  7.15 us (4%)
  local copies, waits for them, and re-layouts  4.08 us (2%)
    all_to_all x1, blocking collectives, body(): got = lax.all_to_all(got[0] + got[1], near_axes, 0, 0)  37.7 us
    all_to_all x1, blocking collectives, body(): got = lax.all_to_all(spread(jnp.sum(got, axis=0), near), near_axes, 0, 0)  29.5 us
    all_to_all x1, blocking collectives, body(): got = lax.all_to_all(strain_part, load_axes, 0, 0)  16.8 us
    all_to_all x1, waiting for transfers between devices, body(): squares = lax.all_to_all(spread(squares, hot_peers), ('zh', 'x', 'c'), 0, 0)  14.1 us
    all_to_all x1, blocking collectives, body(): image = jnp.sum(lax.all_to_all(image_part, load_axes, 0, 0), axis=0)  10.7 us
    all_to_all x1, blocking collectives, body(): lax.all_to_all(spread(jnp.sum(got, axis=0), peers), load_axes, 0, 0)  10.5 us
    all_to_all x1, blocking collectives, body(): image = lax.all_to_all(spread(image, peers), load_axes, 0, 0)  10.4 us
    all_to_all x1, blocking collectives, body(): lax.all_to_all(spread(got, 2), 'c', 0, 0)  9.32 us
  transfers between devices with their start and end apart: 1, of which 1 were waited for; matrix products, arithmetic and copies ran while one was open for 0% of the time, Pallas kernels for 0%

profile of v1, /device:TPU:1, one launch (start us, length us, event | category | flops | bytes accessed | tf_op | source)
XLA Modules:
  0.0 165.6 jit_solution(10467758207121407634)
XLA Ops:
  0.6 0.0 copy-start
  0.6 0.0 copy-start.1
  0.6 3.3 %copy.7 = bf16[64,128,128]{1,0,2:T(8,128)(2,1)S(1)} copy(bf16[64,128,128]{2,1,0:T(8,128)(2,1)} %param.3) | data formatting | bytes 4194304 | tf_op args[0]
  4.0 0.0 copy-done
  4.0 0.0 copy-done.1
  4.0 2.4 %shard_map.50 = (f32[16,16,128]{2,1,0:T(8,128)S(1)}, f32[192,128]{1,0:T(8,128)S(1)}) custom-call(bf16[128,64,128]{2,1,0:T(8,128)(2,1)S(1)} %bitcast.8, bf16[128,1408]{1,0:T(8,128)(2,1)S(1)} %copy-done, f32[64,384]{1,0:T(8,128)S(1)} %copy-done.1), custom_call_target="tpu_custom_call" | custom-call | tf_op jit(solution)/shard_map/pallas_call | solution.py:199
  6.4 16.8 %all_to_all.45 = f32[16,16,128]{2,1,0:T(8,128)S(1)} all-to-all(f32[16,16,128]{2,1,0:T(8,128)S(1)} %get-tuple-element.6), channel_id=1, replica_groups=mesh['zh'=4,'x'=4,'c'=2,'zl'=4,'y'=4] {'zl','y'}, dimensions={0} | all-to-all | bytes 262144 | tf_op jit(solution)/shard_map/all_to_all | solution.py:200
  23.2 10.5 %all_to_all.46.strains_ref = f32[16,16,128]{2,1,0:T(8,128)S(1)} all-to-all(f32[16,16,128]{2,1,0:T(8,128)S(1)} %broadcast_in_dim.10), channel_id=1, replica_groups=mesh['zh'=4,'x'=4,'c'=2,'zl'=4,'y'=4] {'zl','y'}, dimensions={0} | all-to-all | bytes 262144 | tf_op jit(solution)/shard_map/all_to_all | solution.py:201
  33.7 1.7 shard_map.51
  35.4 7.1 %all_to_all.47 = f32[2,16,48,128]{3,2,1,0:T(8,128)S(1)} all-to-all(f32[2,16,48,128]{3,2,1,0:T(8,128)S(1)} %bitcast.13), channel_id=1, replica_groups=mesh['zh'=4,'x'=4,'c'=2,'zl'=4,'y'=4] {'c'}, dimensions={0} | all-to-all | bytes 1572864 | tf_op jit(solution)/shard_map/all_to_all | solution.py:213
  42.5 37.7 %all_to_all.48 = f32[16,48,128]{2,1,0:T(8,128)S(1)} all-to-all(f32[16,48,128]{2,1,0:T(8,128)S(1)} %fusion), channel_id=1, replica_groups=mesh['zh'=4,'x'=4,'c'=2,'zl'=4,'y'=4] {'zh','x'}, dimensions={0} | all-to-all | bytes 786432 | tf_op jit(solution)/shard_map/all_to_all | solution.py:214
  80.3 29.5 %all_to_all.49 = f32[16,48,128]{2,1,0:T(8,128)S(1)} all-to-all(f32[16,48,128]{2,1,0:T(8,128)S(1)} %broadcast_in_dim.11), channel_id=1, replica_groups=mesh['zh'=4,'x'=4,'c'=2,'zl'=4,'y'=4] {'zh','x'}, dimensions={0} | all-to-all | bytes 786432 | tf_op jit(solution)/shard_map/all_to_all | solution.py:215
  109.8 0.1 broadcast_in_dim.12
  109.8 9.3 %all_to_all.50 = f32[2,16,48,128]{3,2,1,0:T(8,128)S(1)} all-to-all(f32[2,16,48,128]{3,2,1,0:T(8,128)S(1)} %broadcast_in_dim.12), channel_id=1, replica_groups=mesh['zh'=4,'x'=4,'c'=2,'zl'=4,'y'=4] {'c'}, dimensions={0} | all-to-all | bytes 1572864 | tf_op jit(solution)/shard_map/all_to_all | solution.py:216
  119.2 1.9 %shard_map.52 = f32[16,16,128]{2,1,0:T(8,128)S(1)} custom-call(bf16[128,64,128]{2,1,0:T(8,128)(2,1)S(1)} %bitcast.10, f32[32,48,128]{2,1,0:T(8,128)S(1)} %bitcast.11), custom_call_target="tpu_custom_call" | custom-call | tf_op jit(solution)/shard_map/pallas_call | solution.py:217
  121.0 10.7 %all_to_all.51 = f32[16,16,128]{2,1,0:T(8,128)S(1)} all-to-all(f32[16,16,128]{2,1,0:T(8,128)S(1)} %shard_map.52), channel_id=1, replica_groups=mesh['zh'=4,'x'=4,'c'=2,'zl'=4,'y'=4] {'zl','y'}, dimensions={0} | all-to-all | bytes 262144 | tf_op jit(solution)/shard_map/all_to_all | solution.py:218
  131.7 0.6 broadcast_in_dim.13
  132.3 7.4 %all-to-all-start.7 = ((f32[32,1,128]{2,1,0:T(1,128)}), f32[32,1,128]{2,1,0:T(1,128)S(1)}, u32[]{:S(2)}, u32[]{:S(2)}) async-start(f32[32,1,128]{2,1,0:T(1,128)} %broadcast_in_dim.13), calls=%async_computation.7 | async-start | bytes 32768 | tf_op jit(solution)/shard_map/all_to_all | solution.py:221
  139.8 14.1 %all-to-all-done.7 = f32[32,1,128]{2,1,0:T(1,128)S(1)} async-done(((f32[32,1,128]{2,1,0:T(1,128)}), f32[32,1,128]{2,1,0:T(1,128)S(1)}, u32[]{:S(2)}, u32[]{:S(2)}) %all-to-all-start.7) | async-done | bytes 16416 | tf_op jit(solution)/shard_map/all_to_all | solution.py:221
  153.9 10.4 %all_to_all.52.image_ref = f32[16,16,128]{2,1,0:T(8,128)S(1)} all-to-all(f32[16,16,128]{2,1,0:T(8,128)S(1)} %broadcast_in_dim.14), channel_id=1, replica_groups=mesh['zh'=4,'x'=4,'c'=2,'zl'=4,'y'=4] {'zl','y'}, dimensions={0} | all-to-all | bytes 262144 | tf_op jit(solution)/shard_map/all_to_all | solution.py:224
  164.4 1.3 shard_map.53
  (11 shorter events, 0.2 us)
Async XLA Ops:
  0.6 3.4 %copy-start = (bf16[128,1408]{1,0:T(8,128)(2,1)S(1)}, bf16[128,1408]{1,0:T(8,128)(2,1)}, u32[]{:S(2)}) copy-start(bf16[128,1408]{1,0:T(8,128)(2,1)} %forces_ref.3) | copy-start | bytes 1081348
  0.6 3.4 %copy-start.1 = (f32[64,384]{1,0:T(8,128)S(1)}, f32[64,384]{1,0:T(8,128)}, u32[]{:S(2)}) copy-start(f32[64,384]{1,0:T(8,128)} %measured_ref.1) | copy-start | bytes 294916
  132.3 21.5 %all-to-all-start.7 = ((f32[32,1,128]{2,1,0:T(1,128)}), f32[32,1,128]{2,1,0:T(1,128)S(1)}, u32[]{:S(2)}, u32[]{:S(2)}) async-start(f32[32,1,128]{2,1,0:T(1,128)} %broadcast_in_dim.13), calls=%async_computation.7 | async-start | bytes 32768 | tf_op jit(solution)/shard_map/all_to_all | solution.py:221

commit v2 on v1

--- a/solution.py
+++ b/solution.py
@@ -94,7 +94,7 @@
     measured_t_ref[:, hots:2 * hots] = measured_t[half:]
 
 
-def gradient_kernel(taps_ref, strains_ref, measured_t_ref, part_ref, residual_ref, packed, padded, windows, weights, total):
+def gradient_kernel(core_ref, taps_ref, strains_ref, measured_t_ref, kept_ref, sent_ref, residual_ref, packed, padded, windows, weights, total):
     hots = taps_ref.shape[1]
     half = SEG_COLS // 2
     unpack_strains(strains_ref, packed)
@@ -122,18 +122,19 @@
                 else:
                     total[cols, :] = piece
                     seen.add(block)
-    chunks = part_ref.shape[0]
-    size = COLS // chunks
-    for chunk in range(chunks):
-        part_ref[chunk, 0:size, :] = total[chunk * size:(chunk + 1) * size, :]
-        part_ref[chunk, size:, :] = jnp.zeros((part_ref.shape[1] - size, LANES), F32)
-
-
-def image_kernel(taps_ref, gradient_ref, part_ref, signal_t, windows, weights, packed):
-    chunks = gradient_ref.shape[0]
-    size = COLS // chunks
-    for chunk in range(chunks):
-        signal_t[chunk * size:(chunk + 1) * size, :] = gradient_ref[chunk, 0:size, :]
+    rows = kept_ref.shape[0]
+    kept_ref[...] = total[pl.ds(pl.multiple_of(core_ref[0] * rows, rows), rows), :]
+    sent_ref[...] = total[pl.ds(pl.multiple_of((1 - core_ref[0]) * rows, rows), rows), :]
+
+
+def join_halves(core_ref, own_ref, other_ref, signal_t):
+    rows = own_ref.shape[0]
+    signal_t[pl.ds(pl.multiple_of(core_ref[0] * rows, rows), rows), :] = own_ref[...]
+    signal_t[pl.ds(pl.multiple_of((1 - core_ref[0]) * rows, rows), rows), :] = other_ref[...]
+
+
+def image_kernel(core_ref, taps_ref, own_ref, other_ref, part_ref, signal_t, windows, weights, packed):
+    join_halves(core_ref, own_ref, other_ref, signal_t)
     result = forward_product(signal_t, taps_ref, windows, weights)
     gradient = signal_t[...]
     squares = jnp.sum(gradient * gradient, axis=0, keepdims=True)
@@ -143,7 +144,7 @@
         part_ref[chunk, size:, :] = jnp.broadcast_to(squares, (part_ref.shape[1] - size, LANES))
 
 
-def update_kernel(forces_ref, gradient_ref, image_ref, residual_ref, forces_out, residual_out, signal_t, packed):
+def update_kernel(core_ref, forces_ref, own_ref, other_ref, image_ref, residual_ref, forces_out, residual_out, signal_t, packed):
     size = (SEG_COLS // 2) // image_ref.shape[0]
     squares = image_ref[0, size:size + 1, :]
     image_squares = jnp.zeros((1, LANES), F32)
@@ -156,35 +157,34 @@
     half = SEG_COLS // 2
     left_t = jnp.concatenate([left[:, 0:hots], left[:, hots:2 * hots]], axis=0)
     residual_out[...] = left_t.T
-    chunks = gradient_ref.shape[0]
-    size = COLS // chunks
-    for chunk in range(chunks):
-        signal_t[chunk * size:(chunk + 1) * size, :] = gradient_ref[chunk, 0:size, :]
+    join_halves(core_ref, own_ref, other_ref, signal_t)
     for block in range(BLOCKS):
         cols = slice(block * LANES, (block + 1) * LANES)
         forces_out[:, cols] = forces_ref[:, cols].astype(F32) + step_size * signal_t[cols, :].T
 
 
-def call(kernel, outs, scratch):
+def call(kernel, outs, scratch, operands):
+    spaces = [pltpu.SMEM if operand.dtype == jnp.int32 else pltpu.VMEM for operand in operands]
     return pl.pallas_call(
         kernel,
         out_shape=outs,
+        in_specs=[pl.BlockSpec(memory_space=space) for space in spaces],
         scratch_shapes=scratch,
         compiler_params=pltpu.CompilerParams(vmem_limit_bytes=VMEM_LIMIT),
-    )
+    )(*operands)
 
 
 def body(response, forces, measured):
     hots, loads, _ = response.shape
-    load_axes, near_axes = ("zl", "y"), ("zh", "x")
+    load_axes = ("zl", "y")
     peers = lax.axis_size(load_axes)
-    near = lax.axis_size(near_axes)
-    hot_peers = near * lax.axis_size("c")
-    half = SEG_COLS // 2
-    chunk_rows = -(-(half // peers + 2) // 8) * 8
-    grad_rows = -(-(COLS // hot_peers) // 8) * 8
+    core = lax.axis_index("c").astype(jnp.int32).reshape(1)
+    half = SEG_COLS // 2
+    rows = half // peers
+    chunk_rows = -(-(rows + 2) // 8) * 8
     part = jax.ShapeDtypeStruct((peers, chunk_rows, LANES), F32)
     packed_shape = jax.ShapeDtypeStruct((half, 2 * hots), F32)
+    core_shape = jax.ShapeDtypeStruct((COLS // 2, loads), F32)
     forward_scratch = [
         pltpu.VMEM((COLS, loads), F32),
         pltpu.VMEM((COLS - LANES, PHASES * loads), BF16),
@@ -195,13 +195,23 @@
     def spread(value, count):
         return jnp.broadcast_to(value[None], (count,) + value.shape)
 
+    def scatter_sum(value, axis):
+        return jnp.sum(lax.all_to_all(value, axis, 0, 0), axis=0)
+
+    def gather(value, axis):
+        return lax.all_to_all(spread(value, lax.axis_size(axis)), axis, 0, 0)
+
+    def swapped(value, axis, pairs):
+        return lax.ppermute(value, axis, pairs + [(b, a) for a, b in pairs])
+
     taps = jnp.transpose(response, (2, 0, 1))
-    strain_part, measured_t = call(strain_kernel, (part, packed_shape), forward_scratch)(taps, forces, measured)
-    got = lax.all_to_all(strain_part, load_axes, 0, 0)
-    strains = lax.all_to_all(spread(jnp.sum(got, axis=0), peers), load_axes, 0, 0)
-    grad_part, residual = call(
+    strain_part, measured_t = call(
+        strain_kernel, (part, packed_shape), forward_scratch, (taps, forces, measured)
+    )
+    strains = gather(scatter_sum(strain_part, load_axes), load_axes)
+    kept, sent, residual = call(
         gradient_kernel,
-        (jax.ShapeDtypeStruct((hot_peers, grad_rows, LANES), F32), packed_shape),
+        (core_shape, core_shape, packed_shape),
         [
             pltpu.VMEM((half, 2 * hots), F32),
             pltpu.VMEM((SEG_COLS + 2 * LANES, 2 * hots), F32),
@@ -209,24 +219,27 @@
             pltpu.VMEM((PHASES * hots, SPANS * loads), BF16),
             pltpu.VMEM((COLS, loads), F32),
         ],
-    )(taps, strains, measured_t)
-    got = lax.all_to_all(grad_part.reshape(2, near, grad_rows, LANES), "c", 0, 0)
-    got = lax.all_to_all(got[0] + got[1], near_axes, 0, 0)
-    got = lax.all_to_all(spread(jnp.sum(got, axis=0), near), near_axes, 0, 0)
-    gradient = lax.all_to_all(spread(got, 2), "c", 0, 0).reshape(hot_peers, grad_rows, LANES)
-    image_part = call(image_kernel, part, forward_scratch)(taps, gradient)
-    image = jnp.sum(lax.all_to_all(image_part, load_axes, 0, 0), axis=0)
-    rows = half // peers
+        (core, taps, strains, measured_t),
+    )
+    cores = [(0, 1)]
+    own = kept + swapped(sent, "c", cores)
+    own = scatter_sum(own.reshape(lax.axis_size("x"), -1, loads), "x")
+    own = own + swapped(own, "zh", [(0, 1), (2, 3)])
+    own = own + swapped(own, "zh", [(1, 2), (3, 0)])
+    own = gather(own, "x").reshape(COLS // 2, loads)
+    other = swapped(own, "c", cores)
+    image_part = call(image_kernel, part, forward_scratch, (core, taps, own, other))
+    image = scatter_sum(image_part, load_axes)
     squares = jnp.sum(image[:rows] * image[:rows], axis=0, keepdims=True)
-    squares = lax.all_to_all(spread(squares, hot_peers), ("zh", "x", "c"), 0, 0)
-    squares = jnp.sum(squares, axis=0)
-    image = jnp.concatenate([image[:rows + 1], squares, image[rows + 2:]], axis=0)
-    image = lax.all_to_all(spread(image, peers), load_axes, 0, 0)
+    squares = squares + swapped(squares, "c", cores)
+    squares = jnp.sum(gather(squares, ("zh", "x")), axis=0)
+    image = gather(jnp.concatenate([image[:rows + 1], squares, image[rows + 2:]], axis=0), load_axes)
     return call(
         update_kernel,
         (jax.ShapeDtypeStruct((loads, COLS), F32), jax.ShapeDtypeStruct((hots, SEG_COLS), F32)),
         [pltpu.VMEM((COLS, loads), F32), pltpu.VMEM((half, 2 * hots), F32)],
-    )(forces, gradient, image, residual)
+        (core, forces, own, other, image, residual),
+    )
 
 
 def solution(mesh):

time: 166 us -> 150 us (0.904)
  blocking collectives: 132 us -> 62.7 us
  starting transfers between devices: 7.4 us -> 36.3 us
  waiting for transfers between devices: 14.1 us -> 37 us
    all_to_all x8 -> x5, blocking collectives: 132 us -> 62.7 us  [the longest x3 43.8 us: scatter_sum(): return jnp.sum(lax.all_to_all(value, axis, 0, 0), axis=0)]
    ppermute x0 -> x5, starting transfers between devices: none -> 27.5 us  [swapped(): return lax.ppermute(value, axis, pairs + [(b, a) for a, b in pairs])]
    ppermute x0 -> x5, waiting for transfers between devices: none -> 15.7 us  [swapped(): return lax.ppermute(value, axis, pairs + [(b, a) for a, b in pairs])]
    all_to_all x1 -> x2, waiting for transfers between devices: 14.1 us -> 21.3 us  [gather(): return lax.all_to_all(spread(value, lax.axis_size(axis)), axis, 0, 0)]
    all_to_all x1 -> x2, starting transfers between devices: 7.4 us -> 8.84 us  [gather(): return lax.all_to_all(spread(value, lax.axis_size(axis)), axis, 0, 0)]
  transfers between devices with their start and end apart: 1 -> 7, of which waited for: 1 -> 7; matrix products, arithmetic and copies ran while one was open for 0% -> 0% of each run, Pallas kernels for 0% -> 0%
where the time goes in v2:
time: 150 us; the launch traced here: 149 us
  blocking collectives  62.7 us (42%)
  waiting for transfers between devices  37 us (25%)
  starting transfers between devices  36.3 us (24%)
  Pallas kernels  7.17 us (5%)
  local copies, waits for them, and re-layouts  4.67 us (3%)
    all_to_all x3, blocking collectives, scatter_sum(): return jnp.sum(lax.all_to_all(value, axis, 0, 0), axis=0)  43.8 us
    ppermute x5, starting transfers between devices, swapped(): return lax.ppermute(value, axis, pairs + [(b, a) for a, b in pairs])  27.5 us
    all_to_all x2, waiting for transfers between devices, gather(): return lax.all_to_all(spread(value, lax.axis_size(axis)), axis, 0, 0)  21.3 us
    all_to_all x2, blocking collectives, gather(): return lax.all_to_all(spread(value, lax.axis_size(axis)), axis, 0, 0)  18.9 us
    ppermute x5, waiting for transfers between devices, swapped(): return lax.ppermute(value, axis, pairs + [(b, a) for a, b in pairs])  15.7 us
    all_to_all x2, starting transfers between devices, gather(): return lax.all_to_all(spread(value, lax.axis_size(axis)), axis, 0, 0)  8.84 us
    pallas_call x4, Pallas kernels, call(): pl.pallas_call(kernel, out_shape=outs, in_specs=[pl.BlockSpec(memory_spac...  7.17 us
    unnamed x5, local copies, waits for them, and re-layouts  3.36 us
  transfers between devices with their start and end apart: 7, of which 7 were waited for; matrix products, arithmetic and copies ran while one was open for 0% of the time, Pallas kernels for 0%

profile of v2, /device:TPU:1, one launch (start us, length us, event | category | flops | bytes accessed | tf_op | source)
XLA Modules:
  0.0 148.8 jit_solution(9093367369239743969)
XLA Ops:
  0.6 0.0 copy-start
  0.6 0.0 copy-start.1
  0.6 3.3 %copy.7 = bf16[64,128,128]{1,0,2:T(8,128)(2,1)S(1)} copy(bf16[64,128,128]{2,1,0:T(8,128)(2,1)} %param.3) | data formatting | bytes 4194304 | tf_op args[0]
  4.0 0.0 copy-done
  4.0 0.0 copy-done.1
  4.0 2.3 %shard_map.50 = (f32[16,16,128]{2,1,0:T(8,128)S(1)}, f32[192,128]{1,0:T(8,128)S(1)}) custom-call(bf16[128,64,128]{2,1,0:T(8,128)(2,1)S(1)} %bitcast.11, bf16[128,1408]{1,0:T(8,128)(2,1)S(1)} %copy-done, f32[64,384]{1,0:T(8,128)S(1)} %copy-done.1), custom_call_target="tpu_custom_call" | custom-call | tf_op jit(solution)/shard_map/pallas_call | solution.py:168
  6.4 16.8 %all_to_all.35 = f32[16,16,128]{2,1,0:T(8,128)S(1)} all-to-all(f32[16,16,128]{2,1,0:T(8,128)S(1)} %get-tuple-element.7), channel_id=1, replica_groups=mesh['zh'=4,'x'=4,'c'=2,'zl'=4,'y'=4] {'zl','y'}, dimensions={0} | all-to-all | bytes 262144 | tf_op jit(solution)/shard_map/all_to_all | solution.py:199
  23.2 0.7 broadcast_in_dim.12
  23.9 3.5 %all-to-all-start.1 = ((f32[16,16,128]{2,1,0:T(8,128)}), f32[16,16,128]{2,1,0:T(8,128)S(1)}, u32[]{:S(2)}, u32[]{:S(2)}) async-start(f32[16,16,128]{2,1,0:T(8,128)} %broadcast_in_dim.12), calls=%async_computation.1 | async-start | bytes 262144 | tf_op jit(solution)/shard_map/all_to_all | solution.py:202
  27.4 7.8 %all-to-all-done.1.strains_ref = f32[16,16,128]{2,1,0:T(8,128)S(1)} async-done(((f32[16,16,128]{2,1,0:T(8,128)}), f32[16,16,128]{2,1,0:T(8,128)S(1)}, u32[]{:S(2)}, u32[]{:S(2)}) %all-to-all-start.1) | async-done | bytes 131104 | tf_op jit(solution)/shard_map/all_to_all | solution.py:202
  35.2 1.6 %shard_map.51 = (f32[704,128]{1,0:T(8,128)S(1)}, f32[704,128]{1,0:T(8,128)S(1)}, f32[192,128]{1,0:T(8,128)S(1)}) custom-call(s32[1]{0:T(128)} %bitcast.core_ref, bf16[128,64,128]{2,1,0:T(8,128)(2,1)S(1)} %bitcast.12, f32[16,16,128]{2,1,0:T(8,128)S(1)} %all-to-all-done.1.strains_ref, f32[192,128]{1,0:T(8,128)S(1)} %get-tuple-element.8.measured_t_ref), custom_call_target="tpu_custom_call" | custom-call | tf_op jit(solution)/shard_map/pallas_call | solution.py:168
  36.8 5.1 %collective-permute-start = (f32[704,128]{1,0:T(8,128)S(1)}, f32[704,128]{1,0:T(8,128)S(1)}, u32[]{:S(2)}, u32[]{:S(2)}) collective-permute-start(f32[704,128]{1,0:T(8,128)S(1)} %get-tuple-element.10), channel_id=1, source_target_pairs={{0,16},{16,0},{1,17},{17,1},{2,18},{18,2},{3,19},{19,3},{4,20},{20... | collective-permute-start | bytes 1081352 | tf_op jit(solution)/shard_map/ppermute | solution.py:205
  41.9 1.3 collective-permute-done
  43.2 0.1 add.12
  43.3 10.8 %all_to_all.36 = f32[4,176,128]{2,1,0:T(8,128)S(1)} all-to-all(f32[4,176,128]{2,1,0:T(8,128)S(1)} %bitcast.17), channel_id=1, replica_groups=mesh['zh'=4,'x'=4,'c'=2,'zl'=4,'y'=4] {'x'}, dimensions={0} | all-to-all | bytes 720896 | tf_op jit(solution)/shard_map/all_to_all | solution.py:199
  54.0 8.8 %collective-permute-start.1 = (f32[176,128]{1,0:T(8,128)S(1)}, f32[176,128]{1,0:T(8,128)S(1)}, u32[]{:S(2)}, u32[]{:S(2)}) collective-permute-start(f32[176,128]{1,0:T(8,128)S(1)} %reduce_sum.48), channel_id=1, source_target_pairs={{0,128},{256,384},{128,0},{384,256},{1,129},{257,385},{129,1},{385... | collective-permute-start | bytes 270344 | tf_op jit(solution)/shard_map/ppermute | solution.py:205
  62.9 8.2 %collective-permute-done.1 = f32[176,128]{1,0:T(8,128)S(1)} collective-permute-done((f32[176,128]{1,0:T(8,128)S(1)}, f32[176,128]{1,0:T(8,128)S(1)}, u32[]{:S(2)}, u32[]{:S(2)}) %collective-permute-start.1) | collective-permute-done | bytes 90144 | tf_op jit(solution)/shard_map/ppermute | solution.py:205
  71.1 5.4 %collective-permute-start.2 = (f32[176,128]{1,0:T(8,128)S(1)}, f32[176,128]{1,0:T(8,128)S(1)}, u32[]{:S(2)}, u32[]{:S(2)}) collective-permute-start(f32[176,128]{1,0:T(8,128)S(1)} %add.13), channel_id=1, source_target_pairs={{128,256},{384,0},{256,128},{0,384},{129,257},{385,1},{257,129},{1... | collective-permute-start | bytes 270344 | tf_op jit(solution)/shard_map/ppermute | solution.py:205
  76.5 4.1 %collective-permute-done.2 = f32[176,128]{1,0:T(8,128)S(1)} collective-permute-done((f32[176,128]{1,0:T(8,128)S(1)}, f32[176,128]{1,0:T(8,128)S(1)}, u32[]{:S(2)}, u32[]{:S(2)}) %collective-permute-start.2) | collective-permute-done | bytes 90144 | tf_op jit(solution)/shard_map/ppermute | solution.py:205
  80.6 8.5 %all_to_all.37 = f32[4,176,128]{2,1,0:T(8,128)S(1)} all-to-all(f32[4,176,128]{2,1,0:T(8,128)S(1)} %broadcast_in_dim.13), channel_id=1, replica_groups=mesh['zh'=4,'x'=4,'c'=2,'zl'=4,'y'=4] {'x'}, dimensions={0} | all-to-all | bytes 720896 | tf_op jit(solution)/shard_map/all_to_all | solution.py:202
  89.1 4.5 %collective-permute-start.3 = (f32[704,128]{1,0:T(8,128)S(1)}, f32[704,128]{1,0:T(8,128)S(1)}, u32[]{:S(2)}, u32[]{:S(2)}) collective-permute-start(f32[704,128]{1,0:T(8,128)S(1)} %bitcast.14), channel_id=1, source_target_pairs={{0,16},{16,0},{1,17},{17,1},{2,18},{18,2},{3,19},{19,3},{4,20},{20... | collective-permute-start | bytes 1081352 | tf_op jit(solution)/shard_map/ppermute | solution.py:205
  93.6 1.3 collective-permute-done.3.other_ref
  94.9 1.8 %shard_map.52 = f32[16,16,128]{2,1,0:T(8,128)S(1)} custom-call(s32[1]{0:T(128)} %bitcast.core_ref, bf16[128,64,128]{2,1,0:T(8,128)(2,1)S(1)} %bitcast.13, f32[704,128]{1,0:T(8,128)S(1)} %bitcast.15, f32[704,128]{1,0:T(8,128)S(1)} %collective-permute-done.3.other_ref), custom_call_target="tpu_custom_call" | custom-call | tf_op jit(solution)/shard_map/pallas_call | solution.py:168
  96.8 16.2 %all_to_all.38 = f32[16,16,128]{2,1,0:T(8,128)S(1)} all-to-all(f32[16,16,128]{2,1,0:T(8,128)S(1)} %shard_map.52), channel_id=1, replica_groups=mesh['zh'=4,'x'=4,'c'=2,'zl'=4,'y'=4] {'zl','y'}, dimensions={0} | all-to-all | bytes 262144 | tf_op jit(solution)/shard_map/all_to_all | solution.py:199
  113.0 3.7 %collective-permute-start.4 = (f32[1,128]{1,0:T(1,128)S(1)}, f32[1,128]{1,0:T(1,128)S(1)}, u32[]{:S(2)}, u32[]{:S(2)}) collective-permute-start(f32[1,128]{1,0:T(1,128)S(1)} %bitcast.21), channel_id=1, source_target_pairs={{0,16},{16,0},{1,17},{17,1},{2,18},{18,2},{3,19},{19,3},{4,20},{20... | collective-permute-start | bytes 1544 | tf_op jit(solution)/shard_map/ppermute | solution.py:205
  116.7 0.8 collective-permute-done.4
  117.5 0.6 broadcast_in_dim.16
  118.1 5.3 %all-to-all-start.5 = ((f32[16,1,128]{2,1,0:T(1,128)}), f32[16,1,128]{2,1,0:T(1,128)S(1)}, u32[]{:S(2)}, u32[]{:S(2)}) async-start(f32[16,1,128]{2,1,0:T(1,128)} %broadcast_in_dim.16), calls=%async_computation.5 | async-start | bytes 16384 | tf_op jit(solution)/shard_map/all_to_all | solution.py:202
  123.4 13.5 %all-to-all-done.5 = f32[16,1,128]{2,1,0:T(1,128)S(1)} async-done(((f32[16,1,128]{2,1,0:T(1,128)}), f32[16,1,128]{2,1,0:T(1,128)S(1)}, u32[]{:S(2)}, u32[]{:S(2)}) %all-to-all-start.5) | async-done | bytes 8224 | tf_op jit(solution)/shard_map/all_to_all | solution.py:202
  137.0 10.5 %all_to_all.39.image_ref = f32[16,16,128]{2,1,0:T(8,128)S(1)} all-to-all(f32[16,16,128]{2,1,0:T(8,128)S(1)} %broadcast_in_dim.34), channel_id=1, replica_groups=mesh['zh'=4,'x'=4,'c'=2,'zl'=4,'y'=4] {'zl','y'}, dimensions={0} | all-to-all | bytes 262144 | tf_op jit(solution)/shard_map/all_to_all | solution.py:202
  147.5 1.3 shard_map.53
  (12 shorter events, 0.2 us)
Async XLA Ops:
  0.6 3.4 %copy-start = (bf16[128,1408]{1,0:T(8,128)(2,1)S(1)}, bf16[128,1408]{1,0:T(8,128)(2,1)}, u32[]{:S(2)}) copy-start(bf16[128,1408]{1,0:T(8,128)(2,1)} %forces_ref.3) | copy-start | bytes 1081348
  0.6 3.4 %copy-start.1 = (f32[64,384]{1,0:T(8,128)S(1)}, f32[64,384]{1,0:T(8,128)}, u32[]{:S(2)}) copy-start(f32[64,384]{1,0:T(8,128)} %measured_ref.1) | copy-start | bytes 294916
  23.9 11.3 %all-to-all-start.1 = ((f32[16,16,128]{2,1,0:T(8,128)}), f32[16,16,128]{2,1,0:T(8,128)S(1)}, u32[]{:S(2)}, u32[]{:S(2)}) async-start(f32[16,16,128]{2,1,0:T(8,128)} %broadcast_in_dim.12), calls=%async_computation.1 | async-start | bytes 262144 | tf_op jit(solution)/shard_map/all_to_all | solution.py:202
  36.8 6.3 %collective-permute-start = (f32[704,128]{1,0:T(8,128)S(1)}, f32[704,128]{1,0:T(8,128)S(1)}, u32[]{:S(2)}, u32[]{:S(2)}) collective-permute-start(f32[704,128]{1,0:T(8,128)S(1)} %get-tuple-element.10), channel_id=1, source_target_pairs={{0,16},{16,0},{1,17},{17,1},{2,18},{18,2},{3,19},{19,3},{4,20},{20... | collective-permute-start | bytes 1081352 | tf_op jit(solution)/shard_map/ppermute | solution.py:205
  54.0 17.0 %collective-permute-start.1 = (f32[176,128]{1,0:T(8,128)S(1)}, f32[176,128]{1,0:T(8,128)S(1)}, u32[]{:S(2)}, u32[]{:S(2)}) collective-permute-start(f32[176,128]{1,0:T(8,128)S(1)} %reduce_sum.48), channel_id=1, source_target_pairs={{0,128},{256,384},{128,0},{384,256},{1,129},{257,385},{129,1},{385... | collective-permute-start | bytes 270344 | tf_op jit(solution)/shard_map/ppermute | solution.py:205
  71.1 9.5 %collective-permute-start.2 = (f32[176,128]{1,0:T(8,128)S(1)}, f32[176,128]{1,0:T(8,128)S(1)}, u32[]{:S(2)}, u32[]{:S(2)}) collective-permute-start(f32[176,128]{1,0:T(8,128)S(1)} %add.13), channel_id=1, source_target_pairs={{128,256},{384,0},{256,128},{0,384},{129,257},{385,1},{257,129},{1... | collective-permute-start | bytes 270344 | tf_op jit(solution)/shard_map/ppermute | solution.py:205
  89.1 5.8 %collective-permute-start.3 = (f32[704,128]{1,0:T(8,128)S(1)}, f32[704,128]{1,0:T(8,128)S(1)}, u32[]{:S(2)}, u32[]{:S(2)}) collective-permute-start(f32[704,128]{1,0:T(8,128)S(1)} %bitcast.14), channel_id=1, source_target_pairs={{0,16},{16,0},{1,17},{17,1},{2,18},{18,2},{3,19},{19,3},{4,20},{20... | collective-permute-start | bytes 1081352 | tf_op jit(solution)/shard_map/ppermute | solution.py:205
  113.0 4.5 %collective-permute-start.4 = (f32[1,128]{1,0:T(1,128)S(1)}, f32[1,128]{1,0:T(1,128)S(1)}, u32[]{:S(2)}, u32[]{:S(2)}) collective-permute-start(f32[1,128]{1,0:T(1,128)S(1)} %bitcast.21), channel_id=1, source_target_pairs={{0,16},{16,0},{1,17},{17,1},{2,18},{18,2},{3,19},{19,3},{4,20},{20... | collective-permute-start | bytes 1544 | tf_op jit(solution)/shard_map/ppermute | solution.py:205
  118.1 18.9 %all-to-all-start.5 = ((f32[16,1,128]{2,1,0:T(1,128)}), f32[16,1,128]{2,1,0:T(1,128)S(1)}, u32[]{:S(2)}, u32[]{:S(2)}) async-start(f32[16,1,128]{2,1,0:T(1,128)} %broadcast_in_dim.16), calls=%async_computation.5 | async-start | bytes 16384 | tf_op jit(solution)/shard_map/all_to_all | solution.py:202

commit v3 on v2

v3 whole, which is shorter than its diff:
```python
import jax
import jax.numpy as jnp
from jax import lax
from jax.experimental import pallas as pl
from jax.experimental.pallas import tpu as pltpu
from jax.sharding import Mesh, PartitionSpec as P

TAPS = 128
SEG = 48
CASES = 8
HIST = 128
STEPS = 176
LANES = 128
PHASES = LANES // CASES
SPANS = TAPS // PHASES
SEG_COLS = SEG * CASES
SEG_BLOCKS = SEG_COLS // LANES
COLS = STEPS * CASES
GROUP = 4
BLOCKS = COLS // LANES
F32 = jnp.float32
BF16 = jnp.bfloat16
VMEM_LIMIT = 40 * 1024 * 1024


def forward_product(signal_t, taps_ref):
    hots = taps_ref.shape[1]
    parts = [None] * SEG_BLOCKS
    for block in range(1, BLOCKS, 2):
        low = max(SPANS - 1 - block, 0)
        high = min(SPANS + 2 - block, SPANS - 1)
        first = block * LANES
        windows = [signal_t[first - CASES * phase:first - CASES * phase + 2 * LANES, :].astype(BF16) for phase in range(PHASES)]
        weights = [
            jnp.concatenate([taps_ref[span * PHASES + phase] for phase in range(PHASES)], axis=1)
            for span in range(low, high + 1)
        ]
        out = lax.dot_general(
            jnp.concatenate(windows, axis=1),
            jnp.concatenate(weights, axis=0),
            (((1,), (1,)), ((), ())),
            preferred_element_type=F32,
        )
        for half in range(2):
            for span in range(low, high + 1):
                target = block + half + span - SPANS
                if 0 <= target < SEG_BLOCKS:
                    piece = out[half * LANES:(half + 1) * LANES, (span - low) * hots:(span - low + 1) * hots]
                    parts[target] = piece if parts[target] is None else parts[target] + piece
    return jnp.concatenate(parts, axis=0)


def pack_strains(value, out_ref, scratch):
    half = SEG_COLS // 2
    hots = value.shape[1]
    scratch[:, 0:hots] = value[0:half]
    scratch[:, hots:2 * hots] = value[half:]
    groups = out_ref.shape[1]
    for group in range(half // GROUP):
        out_ref[group // groups, group % groups] = scratch[group * GROUP:(group + 1) * GROUP, :]


def unpack_strains(chunks_ref, scratch):
    half = SEG_COLS // 2
    groups = half // GROUP // chunks_ref.shape[0]
    for group in range(half // GROUP):
        scratch[group * GROUP:(group + 1) * GROUP, :] = chunks_ref[group // groups, group % groups]


def strain_kernel(taps_ref, forces_ref, measured_ref, part_ref, measured_t_ref, signal_t, packed):
    for block in range(BLOCKS):
        cols = slice(block * LANES, (block + 1) * LANES)
        signal_t[cols, :] = forces_ref[:, cols].astype(F32).T
    result = forward_product(signal_t, taps_ref)
    pack_strains(result, part_ref, packed)
    half = SEG_COLS // 2
    hots = measured_ref.shape[0]
    measured_t = measured_ref[...].T
    measured_t_ref[:, 0:hots] = measured_t[0:half]
    measured_t_ref[:, hots:2 * hots] = measured_t[half:]


def gradient_kernel(core_ref, taps_ref, strains_ref, measured_t_ref, kept_ref, sent_ref, residual_ref, packed, padded, windows, total):
    hots = taps_ref.shape[1]
    half = SEG_COLS // 2
    unpack_strains(strains_ref, packed)
    residual = measured_t_ref[...] - packed[...]
    residual_ref[...] = residual
    padded[...] = jnp.zeros_like(padded)
    for lane, shift in ((0, 0), (hots, CASES)):
        padded[LANES - shift:LANES - shift + half, lane:lane + hots] = residual[:, 0:hots]
        padded[LANES - shift + half:LANES - shift + 2 * half, lane:lane + hots] = residual[:, hots:2 * hots]
    rows = windows.shape[0]
    for pair in range(PHASES // 2):
        first = 2 * CASES * pair
        windows[:, pair * 2 * hots:(pair + 1) * 2 * hots] = padded[first:first + rows, :].astype(BF16)
    seen = set()
    for span in range(0, SPANS, 2):
        weights = [
            jnp.concatenate([taps_ref[span * PHASES + phase], taps_ref[(span + 1) * PHASES + phase]], axis=1)
            for phase in range(PHASES)
        ]
        out = jnp.dot(windows[...], jnp.concatenate(weights, axis=0), preferred_element_type=F32)
        for side in range(2):
            for row in range(rows // LANES):
                block = row - 1 + SPANS - (span + side)
                piece = out[row * LANES:(row + 1) * LANES, side * LANES:(side + 1) * LANES]
                cols = slice(block * LANES, (block + 1) * LANES)
                if block in seen:
                    total[cols, :] += piece
                else:
                    total[cols, :] = piece
                    seen.add(block)
    rows = kept_ref.shape[0]
    kept_ref[...] = total[pl.ds(pl.multiple_of(core_ref[0] * rows, rows), rows), :]
    sent_ref[...] = total[pl.ds(pl.multiple_of((1 - core_ref[0]) * rows, rows), rows), :]


def join_halves(core_ref, own_ref, other_ref, signal_t):
    rows = own_ref.shape[0]
    signal_t[pl.ds(pl.multiple_of(core_ref[0] * rows, rows), rows), :] = own_ref[...]
    signal_t[pl.ds(pl.multiple_of((1 - core_ref[0]) * rows, rows), rows), :] = other_ref[...]


def image_kernel(core_ref, taps_ref, own_ref, other_ref, part_ref, squares_ref, signal_t, packed):
    join_halves(core_ref, own_ref, other_ref, signal_t)
    result = forward_product(signal_t, taps_ref)
    gradient = signal_t[...]
    squares_ref[...] = jnp.sum(gradient * gradient, axis=0, keepdims=True)
    pack_strains(result, part_ref, packed)


def turn_kernel(core_ref, own_ref, other_ref, out_ref, signal_t):
    join_halves(core_ref, own_ref, other_ref, signal_t)
    for block in range(BLOCKS):
        cols = slice(block * LANES, (block + 1) * LANES)
        out_ref[:, cols] = signal_t[cols, :].T


def update_kernel(forces_ref, gradient_ref, image_ref, residual_ref, forces_out, residual_out, packed):
    squares = image_ref[0, image_ref.shape[1] - 1]
    for chunk in range(1, image_ref.shape[0]):
        squares = squares + image_ref[chunk, image_ref.shape[1] - 1]
    squares = jnp.sum(squares, axis=1, keepdims=True)
    step_size = squares[1:2] / squares[0:1]
    unpack_strains(image_ref, packed)
    left = residual_ref[...] - step_size * packed[...]
    hots = residual_out.shape[0]
    left_t = jnp.concatenate([left[:, 0:hots], left[:, hots:2 * hots]], axis=0)
    residual_out[...] = left_t.T
    forces_out[...] = forces_ref[...].astype(F32) + step_size * gradient_ref[...]


def call(kernel, outs, scratch, operands):
    spaces = [pltpu.SMEM if operand.dtype == jnp.int32 else pltpu.VMEM for operand in operands]
    return pl.pallas_call(
        kernel,
        out_shape=outs,
        in_specs=[pl.BlockSpec(memory_space=space) for space in spaces],
        scratch_shapes=scratch,
        compiler_params=pltpu.CompilerParams(vmem_limit_bytes=VMEM_LIMIT),
    )(*operands)


def body(response, forces, measured):
    hots, loads, _ = response.shape
    load_axes = ("zl", "y")
    peers = lax.axis_size(load_axes)
    core = lax.axis_index("c").astype(jnp.int32).reshape(1)
    half = SEG_COLS // 2
    part = jax.ShapeDtypeStruct((peers, half // peers // GROUP, GROUP, LANES), F32)
    packed_shape = jax.ShapeDtypeStruct((half, 2 * hots), F32)
    core_shape = jax.ShapeDtypeStruct((COLS // 2, loads), F32)
    forward_scratch = [
        pltpu.VMEM((COLS, loads), F32),
        pltpu.VMEM((half, 2 * hots), F32),
    ]

    def spread(value, count):
        return jnp.broadcast_to(value[None], (count,) + value.shape)

    def scatter_sum(value, axis):
        return jnp.sum(lax.all_to_all(value, axis, 0, 0), axis=0)

    def gather(value, axis):
        return lax.all_to_all(spread(value, lax.axis_size(axis)), axis, 0, 0)

    def swapped(value, axis, pairs):
        return lax.ppermute(value, axis, pairs + [(b, a) for a, b in pairs])

    taps, core = lax.optimization_barrier((jnp.transpose(response, (2, 0, 1)), core))
    strain_part, measured_t = call(
        strain_kernel, (part, packed_shape), forward_scratch, (taps, forces, measured)
    )
    strains = gather(scatter_sum(strain_part, load_axes), load_axes)
    kept, sent, residual = call(
        gradient_kernel,
        (core_shape, core_shape, packed_shape),
        [
            pltpu.VMEM((half, 2 * hots), F32),
            pltpu.VMEM((SEG_COLS + 2 * LANES, 2 * hots), F32),
            pltpu.VMEM((SEG_COLS + LANES, PHASES * hots), BF16),
            pltpu.VMEM((COLS, loads), F32),
        ],
        (core, taps, strains, measured_t),
    )
    cores = [(0, 1)]
    own = kept + swapped(sent, "c", cores)
    own = scatter_sum(own.reshape(lax.axis_size("x"), -1, loads), "x")
    inner, outer = [(0, 1), (2, 3)], [(1, 2), (3, 0)]
    for even, odd in ((inner, outer), (outer, inner)):
        pairs = [(2 * i, 2 * j) for i, j in even] + [(2 * i + 1, 2 * j + 1) for i, j in odd]
        own = own + swapped(own, ("zh", "c"), pairs)
    own = gather(own, "x").reshape(COLS // 2, loads)
    other = swapped(own, "c", cores)
    image_part, own_squares = call(
        image_kernel, (part, jax.ShapeDtypeStruct((1, loads), F32)), forward_scratch, (core, taps, own, other)
    )
    image = scatter_sum(image_part, load_axes)
    squares = jnp.sum(image * image, axis=(0, 1))[None]
    others = swapped(squares, "c", cores)
    halves = lax.optimization_barrier((own, other, squares))[:2]
    gradient = call(
        turn_kernel,
        jax.ShapeDtypeStruct((loads, COLS), F32),
        [pltpu.VMEM((COLS, loads), F32)],
        (core,) + halves,
    )
    squares, gradient = lax.optimization_barrier((squares + others, gradient))
    squares = jnp.sum(gather(squares, ("zh", "x")), axis=0)
    image, squares, own_squares = lax.optimization_barrier((image, squares, own_squares))
    extra = jnp.concatenate([squares, own_squares] * (GROUP // 2), axis=0)
    image = gather(jnp.concatenate([image, extra[None]], axis=0), load_axes)
    return call(
        update_kernel,
        (jax.ShapeDtypeStruct((loads, COLS), F32), jax.ShapeDtypeStruct((hots, SEG_COLS), F32)),
        [pltpu.VMEM((half, 2 * hots), F32)],
        (forces, gradient, image, residual),
    )


def solution(mesh):
    parts = Mesh(mesh.devices.reshape(4, 4, 2, 4, 4), ("zh", "x", "c", "zl", "y"))
    hot, load = ("zh", "x", "c"), ("zl", "y")
    return jax.shard_map(
        body,
        mesh=parts,
        in_specs=(P(hot, load, None), P(load, None), P(hot, None)),
        out_specs=(P(load, None), P(hot, None)),
        check_vma=False,
    )
```

time: 150 us -> 146 us (0.973)
  blocking collectives: 62.7 us -> 91 us
  waiting for transfers between devices: 37 us -> 11.3 us
  starting transfers between devices: 36.3 us -> 31.6 us
    all_to_all x2 -> x4, blocking collectives: 18.9 us -> 53.5 us  [gather(): return lax.all_to_all(spread(value, lax.axis_size(axis)), axis, 0, 0)]
    all_to_all x2 -> x0, waiting for transfers between devices: 21.3 us -> none  [gather(): return lax.all_to_all(spread(value, lax.axis_size(axis)), axis, 0, 0)]
    all_to_all x2 -> x0, starting transfers between devices: 8.84 us -> none  [gather(): return lax.all_to_all(spread(value, lax.axis_size(axis)), axis, 0, 0)]
    all_to_all x3, blocking collectives: 43.8 us -> 37.5 us  [scatter_sum(): return jnp.sum(lax.all_to_all(value, axis, 0, 0), axis=0)]
    ppermute x5, waiting for transfers between devices: 15.7 us -> 11.3 us  [swapped(): return lax.ppermute(value, axis, pairs + [(b, a) for a, b in pairs])]
    ppermute x5, starting transfers between devices: 27.5 us -> 31.6 us  [swapped(): return lax.ppermute(value, axis, pairs + [(b, a) for a, b in pairs])]
    pallas_call x4 -> x5, Pallas kernels: 7.17 us -> 6.33 us  [call(): pl.pallas_call(kernel, out_shape=outs, in_specs=[pl.BlockSpec(memory_spac...]
  transfers between devices with their start and end apart: 7 -> 5, of which waited for: 7 -> 5; matrix products, arithmetic and copies ran while one was open for 0% -> 0% of each run, Pallas kernels for 0% -> 0%
where the time goes in v3:
time: 146 us; the launch traced here: 145 us
  blocking collectives  91 us (62%)
  starting transfers between devices  31.6 us (22%)
  waiting for transfers between devices  11.3 us (8%)
  Pallas kernels  6.33 us (4%)
  local copies, waits for them, and re-layouts  3.43 us (2%)
    all_to_all x4, blocking collectives, gather(): return lax.all_to_all(spread(value, lax.axis_size(axis)), axis, 0, 0)  53.5 us
    all_to_all x3, blocking collectives, scatter_sum(): return jnp.sum(lax.all_to_all(value, axis, 0, 0), axis=0)  37.5 us
    ppermute x5, starting transfers between devices, swapped(): return lax.ppermute(value, axis, pairs + [(b, a) for a, b in pairs])  31.6 us
    ppermute x5, waiting for transfers between devices, swapped(): return lax.ppermute(value, axis, pairs + [(b, a) for a, b in pairs])  11.3 us
    pallas_call x5, Pallas kernels, call(): pl.pallas_call(kernel, out_shape=outs, in_specs=[pl.BlockSpec(memory_spac...  6.33 us
    unnamed x5, local copies, waits for them, and re-layouts  3.36 us
  transfers between devices with their start and end apart: 5, of which 5 were waited for; matrix products, arithmetic and copies ran while one was open for 0% of the time, Pallas kernels for 0%

profile of v3, /device:TPU:1, one launch (start us, length us, event | category | flops | bytes accessed | tf_op | source)
XLA Modules:
  0.0 144.6 jit_solution(14941714604908901842)
XLA Ops:
  0.6 0.0 copy-start
  0.6 0.0 copy-start.1
  0.7 3.3 %copy.7 = bf16[64,128,128]{1,0,2:T(8,128)(2,1)S(1)} copy(bf16[64,128,128]{2,1,0:T(8,128)(2,1)} %param.3) | data formatting | bytes 4194304 | tf_op args[0]
  4.0 0.0 copy-done
  4.0 0.0 copy-done.1
  4.0 1.7 %shard_map.50 = (f32[16,3,4,128]{3,2,1,0:T(4,128)S(1)}, f32[192,128]{1,0:T(8,128)S(1)}) custom-call(bf16[128,64,128]{2,1,0:T(8,128)(2,1)S(1)} %bitcast.11, bf16[128,1408]{1,0:T(8,128)(2,1)S(1)} %copy-done, f32[64,384]{1,0:T(8,128)S(1)} %copy-done.1), custom_call_target="tpu_custom_call" | custom-call | tf_op jit(solution)/shard_map/pallas_call | solution.py:156
  5.8 16.5 %all_to_all.35 = f32[16,3,4,128]{3,2,1,0:T(4,128)S(1)} all-to-all(f32[16,3,4,128]{3,2,1,0:T(4,128)S(1)} %get-tuple-element.20), channel_id=1, replica_groups=mesh['zh'=4,'x'=4,'c'=2,'zl'=4,'y'=4] {'zl','y'}, dimensions={0} | all-to-all | bytes 196608 | tf_op jit(solution)/shard_map/all_to_all | solution.py:183
  22.3 10.1 %all_to_all.36.strains_ref = f32[16,3,4,128]{3,2,1,0:T(4,128)S(1)} all-to-all(f32[16,3,4,128]{3,2,1,0:T(4,128)S(1)} %broadcast_in_dim.14), channel_id=1, replica_groups=mesh['zh'=4,'x'=4,'c'=2,'zl'=4,'y'=4] {'zl','y'}, dimensions={0} | all-to-all | bytes 196608 | tf_op jit(solution)/shard_map/all_to_all | solution.py:186
  32.4 1.4 %shard_map.51 = (f32[704,128]{1,0:T(8,128)S(1)}, f32[704,128]{1,0:T(8,128)S(1)}, f32[192,128]{1,0:T(8,128)S(1)}) custom-call(s32[1]{0:T(128)} %bitcast.1.core_ref, bf16[128,64,128]{2,1,0:T(8,128)(2,1)S(1)} %bitcast.12, f32[16,3,4,128]{3,2,1,0:T(4,128)S(1)} %all_to_all.36.strains_ref, f32[192,128]{1,0:T(8,128)S(1)} %get-tuple-element.21.measured_t_ref), custom_call_target="tpu_custom_call" | custom-call | tf_op jit(solution)/shard_map/pallas_call | solution.py:156
  33.9 5.1 %collective-permute-start = (f32[704,128]{1,0:T(8,128)S(1)}, f32[704,128]{1,0:T(8,128)S(1)}, u32[]{:S(2)}, u32[]{:S(2)}) collective-permute-start(f32[704,128]{1,0:T(8,128)S(1)} %get-tuple-element.23), channel_id=1, source_target_pairs={{0,16},{16,0},{1,17},{17,1},{2,18},{18,2},{3,19},{19,3},{4,20},{20... | collective-permute-start | bytes 1081352 | tf_op jit(solution)/shard_map/ppermute | solution.py:189
  39.0 1.3 collective-permute-done
  40.4 10.8 %all_to_all.37 = f32[4,176,128]{2,1,0:T(8,128)S(1)} all-to-all(f32[4,176,128]{2,1,0:T(8,128)S(1)} %bitcast.17), channel_id=1, replica_groups=mesh['zh'=4,'x'=4,'c'=2,'zl'=4,'y'=4] {'x'}, dimensions={0} | all-to-all | bytes 720896 | tf_op jit(solution)/shard_map/all_to_all | solution.py:183
  51.2 9.8 %collective-permute-start.1 = (f32[176,128]{1,0:T(8,128)S(1)}, f32[176,128]{1,0:T(8,128)S(1)}, u32[]{:S(2)}, u32[]{:S(2)}) collective-permute-start(f32[176,128]{1,0:T(8,128)S(1)} %reduce_sum.48), channel_id=1, source_target_pairs={{0,128},{256,384},{144,272},{400,16},{128,0},{384,256},{272,144},{... | collective-permute-start | bytes 270344 | tf_op jit(solution)/shard_map/ppermute | solution.py:189
  60.9 3.8 %collective-permute-done.1 = f32[176,128]{1,0:T(8,128)S(1)} collective-permute-done((f32[176,128]{1,0:T(8,128)S(1)}, f32[176,128]{1,0:T(8,128)S(1)}, u32[]{:S(2)}, u32[]{:S(2)}) %collective-permute-start.1) | collective-permute-done | bytes 90144 | tf_op jit(solution)/shard_map/ppermute | solution.py:189
  64.7 6.9 %collective-permute-start.2 = (f32[176,128]{1,0:T(8,128)S(1)}, f32[176,128]{1,0:T(8,128)S(1)}, u32[]{:S(2)}, u32[]{:S(2)}) collective-permute-start(f32[176,128]{1,0:T(8,128)S(1)} %add.13), channel_id=1, source_target_pairs={{128,256},{384,0},{16,144},{272,400},{256,128},{0,384},{144,16},{4... | collective-permute-start | bytes 270344 | tf_op jit(solution)/shard_map/ppermute | solution.py:189
  71.7 4.4 %collective-permute-done.2 = f32[176,128]{1,0:T(8,128)S(1)} collective-permute-done((f32[176,128]{1,0:T(8,128)S(1)}, f32[176,128]{1,0:T(8,128)S(1)}, u32[]{:S(2)}, u32[]{:S(2)}) %collective-permute-start.2) | collective-permute-done | bytes 90144 | tf_op jit(solution)/shard_map/ppermute | solution.py:189
  76.2 8.4 %all_to_all.38 = f32[4,176,128]{2,1,0:T(8,128)S(1)} all-to-all(f32[4,176,128]{2,1,0:T(8,128)S(1)} %broadcast_in_dim.15), channel_id=1, replica_groups=mesh['zh'=4,'x'=4,'c'=2,'zl'=4,'y'=4] {'x'}, dimensions={0} | all-to-all | bytes 720896 | tf_op jit(solution)/shard_map/all_to_all | solution.py:186
  84.6 6.1 %collective-permute-start.3 = (f32[704,128]{1,0:T(8,128)S(1)}, f32[704,128]{1,0:T(8,128)S(1)}, u32[]{:S(2)}, u32[]{:S(2)}) collective-permute-start(f32[704,128]{1,0:T(8,128)S(1)} %bitcast.14), channel_id=1, source_target_pairs={{0,16},{16,0},{1,17},{17,1},{2,18},{18,2},{3,19},{19,3},{4,20},{20... | collective-permute-start | bytes 1081352 | tf_op jit(solution)/shard_map/ppermute | solution.py:189
  90.7 1.3 collective-permute-done.3.other_ref
  92.0 1.7 %shard_map.52 = (f32[16,3,4,128]{3,2,1,0:T(4,128)S(1)}, f32[1,128]{1,0:T(1,128)S(1)}) custom-call(s32[1]{0:T(128)} %bitcast.1.core_ref, bf16[128,64,128]{2,1,0:T(8,128)(2,1)S(1)} %bitcast.13, f32[704,128]{1,0:T(8,128)S(1)} %bitcast.15, f32[704,128]{1,0:T(8,128)S(1)} %collective-permute-done.3.other_ref), custom_call_target="tpu_custom_call" | custom-call | tf_op jit(solution)/shard_map/pallas_call | solution.py:156
  93.7 10.2 %all_to_all.39 = f32[16,3,4,128]{3,2,1,0:T(4,128)S(1)} all-to-all(f32[16,3,4,128]{3,2,1,0:T(4,128)S(1)} %get-tuple-element.24), channel_id=1, replica_groups=mesh['zh'=4,'x'=4,'c'=2,'zl'=4,'y'=4] {'zl','y'}, dimensions={0} | all-to-all | bytes 196608 | tf_op jit(solution)/shard_map/all_to_all | solution.py:183
  103.9 3.7 %collective-permute-start.4 = (f32[1,128]{1,0:T(1,128)S(1)}, f32[1,128]{1,0:T(1,128)S(1)}, u32[]{:S(2)}, u32[]{:S(2)}) collective-permute-start(f32[1,128]{1,0:T(1,128)S(1)} %bitcast.21), channel_id=1, source_target_pairs={{0,16},{16,0},{1,17},{17,1},{2,18},{18,2},{3,19},{19,3},{4,20},{20... | collective-permute-start | bytes 1544 | tf_op jit(solution)/shard_map/ppermute | solution.py:189
  107.6 0.3 shard_map.53.gradient_ref
  108.0 0.5 collective-permute-done.4
  108.5 24.6 %all_to_all.40 = f32[16,1,128]{2,1,0:T(1,128)S(1)} all-to-all(f32[16,1,128]{2,1,0:T(1,128)S(1)} %broadcast_in_dim.36), channel_id=1, replica_groups=mesh['zh'=4,'x'=4,'c'=2,'zl'=4,'y'=4] {'zh','x'}, dimensions={0} | all-to-all | bytes 16384 | tf_op jit(solution)/shard_map/all_to_all | solution.py:186
  133.1 10.4 %all_to_all.41.image_ref = f32[16,4,4,128]{3,2,1,0:T(4,128)S(1)} all-to-all(f32[16,4,4,128]{3,2,1,0:T(4,128)S(1)} %broadcast_in_dim.38), channel_id=1, replica_groups=mesh['zh'=4,'x'=4,'c'=2,'zl'=4,'y'=4] {'zl','y'}, dimensions={0} | all-to-all | bytes 262144 | tf_op jit(solution)/shard_map/all_to_all | solution.py:186
  143.5 1.1 shard_map.54
  (15 shorter events, 0.3 us)
Async XLA Ops:
  0.6 3.4 %copy-start = (bf16[128,1408]{1,0:T(8,128)(2,1)S(1)}, bf16[128,1408]{1,0:T(8,128)(2,1)}, u32[]{:S(2)}) copy-start(bf16[128,1408]{1,0:T(8,128)(2,1)} %forces_ref.3) | copy-start | bytes 1081348
  0.6 3.4 %copy-start.1 = (f32[64,384]{1,0:T(8,128)S(1)}, f32[64,384]{1,0:T(8,128)}, u32[]{:S(2)}) copy-start(f32[64,384]{1,0:T(8,128)} %measured_ref.1) | copy-start | bytes 294916
  33.9 6.4 %collective-permute-start = (f32[704,128]{1,0:T(8,128)S(1)}, f32[704,128]{1,0:T(8,128)S(1)}, u32[]{:S(2)}, u32[]{:S(2)}) collective-permute-start(f32[704,128]{1,0:T(8,128)S(1)} %get-tuple-element.23), channel_id=1, source_target_pairs={{0,16},{16,0},{1,17},{17,1},{2,18},{18,2},{3,19},{19,3},{4,20},{20... | collective-permute-start | bytes 1081352 | tf_op jit(solution)/shard_map/ppermute | solution.py:189
  51.2 13.6 %collective-permute-start.1 = (f32[176,128]{1,0:T(8,128)S(1)}, f32[176,128]{1,0:T(8,128)S(1)}, u32[]{:S(2)}, u32[]{:S(2)}) collective-permute-start(f32[176,128]{1,0:T(8,128)S(1)} %reduce_sum.48), channel_id=1, source_target_pairs={{0,128},{256,384},{144,272},{400,16},{128,0},{384,256},{272,144},{... | collective-permute-start | bytes 270344 | tf_op jit(solution)/shard_map/ppermute | solution.py:189
  64.7 11.4 %collective-permute-start.2 = (f32[176,128]{1,0:T(8,128)S(1)}, f32[176,128]{1,0:T(8,128)S(1)}, u32[]{:S(2)}, u32[]{:S(2)}) collective-permute-start(f32[176,128]{1,0:T(8,128)S(1)} %add.13), channel_id=1, source_target_pairs={{128,256},{384,0},{16,144},{272,400},{256,128},{0,384},{144,16},{4... | collective-permute-start | bytes 270344 | tf_op jit(solution)/shard_map/ppermute | solution.py:189
  84.6 7.4 %collective-permute-start.3 = (f32[704,128]{1,0:T(8,128)S(1)}, f32[704,128]{1,0:T(8,128)S(1)}, u32[]{:S(2)}, u32[]{:S(2)}) collective-permute-start(f32[704,128]{1,0:T(8,128)S(1)} %bitcast.14), channel_id=1, source_target_pairs={{0,16},{16,0},{1,17},{17,1},{2,18},{18,2},{3,19},{19,3},{4,20},{20... | collective-permute-start | bytes 1081352 | tf_op jit(solution)/shard_map/ppermute | solution.py:189
  103.9 4.5 %collective-permute-start.4 = (f32[1,128]{1,0:T(1,128)S(1)}, f32[1,128]{1,0:T(1,128)S(1)}, u32[]{:S(2)}, u32[]{:S(2)}) collective-permute-start(f32[1,128]{1,0:T(1,128)S(1)} %bitcast.21), channel_id=1, source_target_pairs={{0,16},{16,0},{1,17},{17,1},{2,18},{18,2},{3,19},{19,3},{4,20},{20... | collective-permute-start | bytes 1544 | tf_op jit(solution)/shard_map/ppermute | solution.py:189

commit v4 on v3

--- a/solution.py
+++ b/solution.py
@@ -80,7 +80,7 @@
     measured_t_ref[:, hots:2 * hots] = measured_t[half:]
 
 
-def gradient_kernel(core_ref, taps_ref, strains_ref, measured_t_ref, kept_ref, sent_ref, residual_ref, packed, padded, windows, total):
+def gradient_kernel(taps_ref, strains_ref, measured_t_ref, part_ref, residual_ref, packed, padded, windows):
     hots = taps_ref.shape[1]
     half = SEG_COLS // 2
     unpack_strains(strains_ref, packed)
@@ -107,13 +107,10 @@
                 piece = out[row * LANES:(row + 1) * LANES, side * LANES:(side + 1) * LANES]
                 cols = slice(block * LANES, (block + 1) * LANES)
                 if block in seen:
-                    total[cols, :] += piece
+                    part_ref[cols, :] += piece
                 else:
-                    total[cols, :] = piece
+                    part_ref[cols, :] = piece
                     seen.add(block)
-    rows = kept_ref.shape[0]
-    kept_ref[...] = total[pl.ds(pl.multiple_of(core_ref[0] * rows, rows), rows), :]
-    sent_ref[...] = total[pl.ds(pl.multiple_of((1 - core_ref[0]) * rows, rows), rows), :]
 
 
 def join_halves(core_ref, own_ref, other_ref, signal_t):
@@ -130,14 +127,7 @@
     pack_strains(result, part_ref, packed)
 
 
-def turn_kernel(core_ref, own_ref, other_ref, out_ref, signal_t):
-    join_halves(core_ref, own_ref, other_ref, signal_t)
-    for block in range(BLOCKS):
-        cols = slice(block * LANES, (block + 1) * LANES)
-        out_ref[:, cols] = signal_t[cols, :].T
-
-
-def update_kernel(forces_ref, gradient_ref, image_ref, residual_ref, forces_out, residual_out, packed):
+def update_kernel(core_ref, forces_ref, own_ref, other_ref, image_ref, residual_ref, forces_out, residual_out, signal_t, packed):
     squares = image_ref[0, image_ref.shape[1] - 1]
     for chunk in range(1, image_ref.shape[0]):
         squares = squares + image_ref[chunk, image_ref.shape[1] - 1]
@@ -148,7 +138,10 @@
     hots = residual_out.shape[0]
     left_t = jnp.concatenate([left[:, 0:hots], left[:, hots:2 * hots]], axis=0)
     residual_out[...] = left_t.T
-    forces_out[...] = forces_ref[...].astype(F32) + step_size * gradient_ref[...]
+    join_halves(core_ref, own_ref, other_ref, signal_t)
+    for block in range(BLOCKS):
+        cols = slice(block * LANES, (block + 1) * LANES)
+        forces_out[:, cols] = forces_ref[:, cols].astype(F32) + step_size * signal_t[cols, :].T
 
 
 def call(kernel, outs, scratch, operands):
@@ -170,7 +163,6 @@
     half = SEG_COLS // 2
     part = jax.ShapeDtypeStruct((peers, half // peers // GROUP, GROUP, LANES), F32)
     packed_shape = jax.ShapeDtypeStruct((half, 2 * hots), F32)
-    core_shape = jax.ShapeDtypeStruct((COLS // 2, loads), F32)
     forward_scratch = [
         pltpu.VMEM((COLS, loads), F32),
         pltpu.VMEM((half, 2 * hots), F32),
@@ -193,20 +185,19 @@
         strain_kernel, (part, packed_shape), forward_scratch, (taps, forces, measured)
     )
     strains = gather(scatter_sum(strain_part, load_axes), load_axes)
-    kept, sent, residual = call(
+    gradient_part, residual = call(
         gradient_kernel,
-        (core_shape, core_shape, packed_shape),
+        (jax.ShapeDtypeStruct((COLS, loads), F32), packed_shape),
         [
             pltpu.VMEM((half, 2 * hots), F32),
             pltpu.VMEM((SEG_COLS + 2 * LANES, 2 * hots), F32),
             pltpu.VMEM((SEG_COLS + LANES, PHASES * hots), BF16),
-            pltpu.VMEM((COLS, loads), F32),
         ],
-        (core, taps, strains, measured_t),
+        (taps, strains, measured_t),
     )
     cores = [(0, 1)]
-    own = kept + swapped(sent, "c", cores)
-    own = scatter_sum(own.reshape(lax.axis_size("x"), -1, loads), "x")
+    near = ("c", "x")
+    own = scatter_sum(gradient_part.reshape(lax.axis_size(near), -1, loads), near)
     inner, outer = [(0, 1), (2, 3)], [(1, 2), (3, 0)]
     for even, odd in ((inner, outer), (outer, inner)):
         pairs = [(2 * i, 2 * j) for i, j in even] + [(2 * i + 1, 2 * j + 1) for i, j in odd]
@@ -218,24 +209,15 @@
     )
     image = scatter_sum(image_part, load_axes)
     squares = jnp.sum(image * image, axis=(0, 1))[None]
-    others = swapped(squares, "c", cores)
-    halves = lax.optimization_barrier((own, other, squares))[:2]
-    gradient = call(
-        turn_kernel,
-        jax.ShapeDtypeStruct((loads, COLS), F32),
-        [pltpu.VMEM((COLS, loads), F32)],
-        (core,) + halves,
-    )
-    squares, gradient = lax.optimization_barrier((squares + others, gradient))
-    squares = jnp.sum(gather(squares, ("zh", "x")), axis=0)
+    squares = jnp.sum(gather(squares, ("zh", "x", "c")), axis=0)
     image, squares, own_squares = lax.optimization_barrier((image, squares, own_squares))
     extra = jnp.concatenate([squares, own_squares] * (GROUP // 2), axis=0)
     image = gather(jnp.concatenate([image, extra[None]], axis=0), load_axes)
     return call(
         update_kernel,
         (jax.ShapeDtypeStruct((loads, COLS), F32), jax.ShapeDtypeStruct((hots, SEG_COLS), F32)),
-        [pltpu.VMEM((half, 2 * hots), F32)],
-        (forces, gradient, image, residual),
+        [pltpu.VMEM((COLS, loads), F32), pltpu.VMEM((half, 2 * hots), F32)],
+        (core, forces, own, other, image, residual),
     )
 
 

time: 146 us -> 143 us (0.979)
  blocking collectives: 91 us -> 99.9 us
  starting transfers between devices: 31.6 us -> 22.8 us
  waiting for transfers between devices: 11.3 us -> 9.08 us
    ppermute x5 -> x3, starting transfers between devices: 31.6 us -> 22.8 us  [swapped(): return lax.ppermute(value, axis, pairs + [(b, a) for a, b in pairs])]
    all_to_all x3, blocking collectives: 37.5 us -> 45.5 us  [scatter_sum(): return jnp.sum(lax.all_to_all(value, axis, 0, 0), axis=0)]
    ppermute x5 -> x3, waiting for transfers between devices: 11.3 us -> 9.08 us  [swapped(): return lax.ppermute(value, axis, pairs + [(b, a) for a, b in pairs])]
    pallas_call x5 -> x4, Pallas kernels: 6.33 us -> 6.28 us  [call(): pl.pallas_call(kernel, out_shape=outs, in_specs=[pl.BlockSpec(memory_spac...]
  transfers between devices with their start and end apart: 5 -> 3, of which waited for: 5 -> 3; matrix products, arithmetic and copies ran while one was open for 0% -> 0% of each run, Pallas kernels for 0% -> 0%
where the time goes in v4:
time: 143 us; the launch traced here: 142 us
  blocking collectives  99.9 us (70%)
  starting transfers between devices  22.8 us (16%)
  waiting for transfers between devices  9.08 us (6%)
  Pallas kernels  6.28 us (4%)
  local copies, waits for them, and re-layouts  3.43 us (2%)
    all_to_all x4, blocking collectives, gather(): return lax.all_to_all(spread(value, lax.axis_size(axis)), axis, 0, 0)  54.4 us
    all_to_all x3, blocking collectives, scatter_sum(): return jnp.sum(lax.all_to_all(value, axis, 0, 0), axis=0)  45.5 us
    ppermute x3, starting transfers between devices, swapped(): return lax.ppermute(value, axis, pairs + [(b, a) for a, b in pairs])  22.8 us
    ppermute x3, waiting for transfers between devices, swapped(): return lax.ppermute(value, axis, pairs + [(b, a) for a, b in pairs])  9.08 us
    pallas_call x4, Pallas kernels, call(): pl.pallas_call(kernel, out_shape=outs, in_specs=[pl.BlockSpec(memory_spac...  6.28 us
    unnamed x5, local copies, waits for them, and re-layouts  3.36 us
  transfers between devices with their start and end apart: 3, of which 3 were waited for; matrix products, arithmetic and copies ran while one was open for 0% of the time, Pallas kernels for 0%

profile of v4, /device:TPU:1, one launch (start us, length us, event | category | flops | bytes accessed | tf_op | source)
XLA Modules:
  0.0 142.4 jit_solution(12932617710521350612)
XLA Ops:
  0.6 0.0 copy-start
  0.6 0.0 copy-start.1
  0.7 3.3 %copy.7 = bf16[64,128,128]{1,0,2:T(8,128)(2,1)S(1)} copy(bf16[64,128,128]{2,1,0:T(8,128)(2,1)} %param.3) | data formatting | bytes 4194304 | tf_op args[0]
  4.0 0.0 copy-done
  4.0 0.0 copy-done.1
  4.0 1.7 %shard_map.50 = (f32[16,3,4,128]{3,2,1,0:T(4,128)S(1)}, f32[192,128]{1,0:T(8,128)S(1)}) custom-call(bf16[128,64,128]{2,1,0:T(8,128)(2,1)S(1)} %bitcast.8, bf16[128,1408]{1,0:T(8,128)(2,1)S(1)} %copy-done, f32[64,384]{1,0:T(8,128)S(1)} %copy-done.1), custom_call_target="tpu_custom_call" | custom-call | tf_op jit(solution)/shard_map/pallas_call | solution.py:149
  5.8 16.5 %all_to_all.35 = f32[16,3,4,128]{3,2,1,0:T(4,128)S(1)} all-to-all(f32[16,3,4,128]{3,2,1,0:T(4,128)S(1)} %get-tuple-element.15), channel_id=1, replica_groups=mesh['zh'=4,'x'=4,'c'=2,'zl'=4,'y'=4] {'zl','y'}, dimensions={0} | all-to-all | bytes 196608 | tf_op jit(solution)/shard_map/all_to_all | solution.py:175
  22.3 10.1 %all_to_all.36.strains_ref = f32[16,3,4,128]{3,2,1,0:T(4,128)S(1)} all-to-all(f32[16,3,4,128]{3,2,1,0:T(4,128)S(1)} %broadcast_in_dim.10), channel_id=1, replica_groups=mesh['zh'=4,'x'=4,'c'=2,'zl'=4,'y'=4] {'zl','y'}, dimensions={0} | all-to-all | bytes 196608 | tf_op jit(solution)/shard_map/all_to_all | solution.py:178
  32.4 1.4 shard_map.51
  33.8 18.8 %all_to_all.37 = f32[8,176,128]{2,1,0:T(8,128)S(1)} all-to-all(f32[8,176,128]{2,1,0:T(8,128)S(1)} %bitcast.14), channel_id=1, replica_groups=mesh['zh'=4,'x'=4,'c'=2,'zl'=4,'y'=4] {'c','x'}, dimensions={0} | all-to-all | bytes 1441792 | tf_op jit(solution)/shard_map/all_to_all | solution.py:175
  52.7 9.8 %collective-permute-start = (f32[176,128]{1,0:T(8,128)S(1)}, f32[176,128]{1,0:T(8,128)S(1)}, u32[]{:S(2)}, u32[]{:S(2)}) collective-permute-start(f32[176,128]{1,0:T(8,128)S(1)} %reduce_sum.48), channel_id=1, source_target_pairs={{0,128},{256,384},{144,272},{400,16},{128,0},{384,256},{272,144},{... | collective-permute-start | bytes 270344 | tf_op jit(solution)/shard_map/ppermute | solution.py:181
  62.5 3.5 %collective-permute-done = f32[176,128]{1,0:T(8,128)S(1)} collective-permute-done((f32[176,128]{1,0:T(8,128)S(1)}, f32[176,128]{1,0:T(8,128)S(1)}, u32[]{:S(2)}, u32[]{:S(2)}) %collective-permute-start) | collective-permute-done | bytes 90144 | tf_op jit(solution)/shard_map/ppermute | solution.py:181
  66.0 7.1 %collective-permute-start.1 = (f32[176,128]{1,0:T(8,128)S(1)}, f32[176,128]{1,0:T(8,128)S(1)}, u32[]{:S(2)}, u32[]{:S(2)}) collective-permute-start(f32[176,128]{1,0:T(8,128)S(1)} %add.6), channel_id=1, source_target_pairs={{128,256},{384,0},{16,144},{272,400},{256,128},{0,384},{144,16},{4... | collective-permute-start | bytes 270344 | tf_op jit(solution)/shard_map/ppermute | solution.py:181
  73.1 4.3 %collective-permute-done.1 = f32[176,128]{1,0:T(8,128)S(1)} collective-permute-done((f32[176,128]{1,0:T(8,128)S(1)}, f32[176,128]{1,0:T(8,128)S(1)}, u32[]{:S(2)}, u32[]{:S(2)}) %collective-permute-start.1) | collective-permute-done | bytes 90144 | tf_op jit(solution)/shard_map/ppermute | solution.py:181
  77.5 8.4 %all_to_all.38 = f32[4,176,128]{2,1,0:T(8,128)S(1)} all-to-all(f32[4,176,128]{2,1,0:T(8,128)S(1)} %broadcast_in_dim.11), channel_id=1, replica_groups=mesh['zh'=4,'x'=4,'c'=2,'zl'=4,'y'=4] {'x'}, dimensions={0} | all-to-all | bytes 720896 | tf_op jit(solution)/shard_map/all_to_all | solution.py:178
  85.9 5.9 %collective-permute-start.2 = (f32[704,128]{1,0:T(8,128)S(1)}, f32[704,128]{1,0:T(8,128)S(1)}, u32[]{:S(2)}, u32[]{:S(2)}) collective-permute-start(f32[704,128]{1,0:T(8,128)S(1)} %bitcast.11), channel_id=1, source_target_pairs={{0,16},{16,0},{1,17},{17,1},{2,18},{18,2},{3,19},{19,3},{4,20},{20... | collective-permute-start | bytes 1081352 | tf_op jit(solution)/shard_map/ppermute | solution.py:181
  91.8 1.3 collective-permute-done.2.other_ref
  93.1 1.7 %shard_map.52 = (f32[16,3,4,128]{3,2,1,0:T(4,128)S(1)}, f32[1,128]{1,0:T(1,128)S(1)}) custom-call(s32[1]{0:T(128)} %bitcast.1.core_ref, bf16[128,64,128]{2,1,0:T(8,128)(2,1)S(1)} %bitcast.10, f32[704,128]{1,0:T(8,128)S(1)} %bitcast.12, f32[704,128]{1,0:T(8,128)S(1)} %collective-permute-done.2.other_ref), custom_call_target="tpu_custom_call" | custom-call | tf_op jit(solution)/shard_map/pallas_call | solution.py:149
  94.8 10.1 %all_to_all.39 = f32[16,3,4,128]{3,2,1,0:T(4,128)S(1)} all-to-all(f32[16,3,4,128]{3,2,1,0:T(4,128)S(1)} %get-tuple-element.18), channel_id=1, replica_groups=mesh['zh'=4,'x'=4,'c'=2,'zl'=4,'y'=4] {'zl','y'}, dimensions={0} | all-to-all | bytes 196608 | tf_op jit(solution)/shard_map/all_to_all | solution.py:175
  105.0 25.5 %all_to_all.40 = f32[32,1,128]{2,1,0:T(1,128)S(1)} all-to-all(f32[32,1,128]{2,1,0:T(1,128)S(1)} %broadcast_in_dim.12), channel_id=1, replica_groups=mesh['zh'=4,'x'=4,'c'=2,'zl'=4,'y'=4] {'zh','x','c'}, dimensions={0} | all-to-all | bytes 32768 | tf_op jit(solution)/shard_map/all_to_all | solution.py:178
  130.6 10.4 %all_to_all.41.image_ref = f32[16,4,4,128]{3,2,1,0:T(4,128)S(1)} all-to-all(f32[16,4,4,128]{3,2,1,0:T(4,128)S(1)} %broadcast_in_dim.14), channel_id=1, replica_groups=mesh['zh'=4,'x'=4,'c'=2,'zl'=4,'y'=4] {'zl','y'}, dimensions={0} | all-to-all | bytes 262144 | tf_op jit(solution)/shard_map/all_to_all | solution.py:178
  140.9 1.4 %shard_map.53 = (f32[128,1408]{1,0:T(8,128)}, f32[64,384]{1,0:T(8,128)}) custom-call(s32[1]{0:T(128)} %bitcast.1.core_ref, bf16[128,1408]{1,0:T(8,128)(2,1)S(1)} %copy-done, f32[704,128]{1,0:T(8,128)S(1)} %bitcast.13, f32[704,128]{1,0:T(8,128)S(1)} %collective-permute-done.2.other_ref, f32[16,4,4,128]{3,2,1,0:T(4,128)S(1)} %all_to_all.41.image_ref, ...), custom_call_target="tpu_custom_call" | custom-call | tf_op jit(solution)/shard_map/pallas_call | solution.py:149
  (13 shorter events, 0.3 us)
Async XLA Ops:
  0.6 3.4 %copy-start = (bf16[128,1408]{1,0:T(8,128)(2,1)S(1)}, bf16[128,1408]{1,0:T(8,128)(2,1)}, u32[]{:S(2)}) copy-start(bf16[128,1408]{1,0:T(8,128)(2,1)} %forces_ref.3) | copy-start | bytes 1081348
  0.6 3.4 %copy-start.1 = (f32[64,384]{1,0:T(8,128)S(1)}, f32[64,384]{1,0:T(8,128)}, u32[]{:S(2)}) copy-start(f32[64,384]{1,0:T(8,128)} %measured_ref.1) | copy-start | bytes 294916
  52.7 13.2 %collective-permute-start = (f32[176,128]{1,0:T(8,128)S(1)}, f32[176,128]{1,0:T(8,128)S(1)}, u32[]{:S(2)}, u32[]{:S(2)}) collective-permute-start(f32[176,128]{1,0:T(8,128)S(1)} %reduce_sum.48), channel_id=1, source_target_pairs={{0,128},{256,384},{144,272},{400,16},{128,0},{384,256},{272,144},{... | collective-permute-start | bytes 270344 | tf_op jit(solution)/shard_map/ppermute | solution.py:181
  66.0 11.4 %collective-permute-start.1 = (f32[176,128]{1,0:T(8,128)S(1)}, f32[176,128]{1,0:T(8,128)S(1)}, u32[]{:S(2)}, u32[]{:S(2)}) collective-permute-start(f32[176,128]{1,0:T(8,128)S(1)} %add.6), channel_id=1, source_target_pairs={{128,256},{384,0},{16,144},{272,400},{256,128},{0,384},{144,16},{4... | collective-permute-start | bytes 270344 | tf_op jit(solution)/shard_map/ppermute | solution.py:181
  85.9 7.2 %collective-permute-start.2 = (f32[704,128]{1,0:T(8,128)S(1)}, f32[704,128]{1,0:T(8,128)S(1)}, u32[]{:S(2)}, u32[]{:S(2)}) collective-permute-start(f32[704,128]{1,0:T(8,128)S(1)} %bitcast.11), channel_id=1, source_target_pairs={{0,16},{16,0},{1,17},{17,1},{2,18},{18,2},{3,19},{19,3},{4,20},{20... | collective-permute-start | bytes 1081352 | tf_op jit(solution)/shard_map/ppermute | solution.py:181

commit v5 on v4

--- a/solution.py
+++ b/solution.py
@@ -157,7 +157,7 @@
 
 def body(response, forces, measured):
     hots, loads, _ = response.shape
-    load_axes = ("zl", "y")
+    load_axes = ("y", "zl")
     peers = lax.axis_size(load_axes)
     core = lax.axis_index("c").astype(jnp.int32).reshape(1)
     half = SEG_COLS // 2

time: 143 us -> 142 us (level)
  no operation moved by 1% of the time
where the time goes in v5:
time: 142 us; the launch traced here: 141 us
  blocking collectives  99.5 us (70%)
  starting transfers between devices  22.3 us (16%)
  waiting for transfers between devices  8.89 us (6%)
  Pallas kernels  6.28 us (4%)
  local copies, waits for them, and re-layouts  3.43 us (2%)
    all_to_all x4, blocking collectives, gather(): return lax.all_to_all(spread(value, lax.axis_size(axis)), axis, 0, 0)  54.1 us
    all_to_all x3, blocking collectives, scatter_sum(): return jnp.sum(lax.all_to_all(value, axis, 0, 0), axis=0)  45.4 us
    ppermute x3, starting transfers between devices, swapped(): return lax.ppermute(value, axis, pairs + [(b, a) for a, b in pairs])  22.3 us
    ppermute x3, waiting for transfers between devices, swapped(): return lax.ppermute(value, axis, pairs + [(b, a) for a, b in pairs])  8.89 us
    pallas_call x4, Pallas kernels, call(): pl.pallas_call(kernel, out_shape=outs, in_specs=[pl.BlockSpec(memory_spac...  6.28 us
    unnamed x5, local copies, waits for them, and re-layouts  3.36 us
  transfers between devices with their start and end apart: 3, of which 3 were waited for; matrix products, arithmetic and copies ran while one was open for 0% of the time, Pallas kernels for 0%

profile of v5, /device:TPU:1, one launch (start us, length us, event | category | flops | bytes accessed | tf_op | source)
XLA Modules:
  0.0 141.4 jit_solution(457176037343047251)
XLA Ops:
  0.6 0.0 copy-start
  0.6 0.0 copy-start.1
  0.7 3.3 %copy.7 = bf16[64,128,128]{1,0,2:T(8,128)(2,1)S(1)} copy(bf16[64,128,128]{2,1,0:T(8,128)(2,1)} %param.3) | data formatting | bytes 4194304 | tf_op args[0]
  4.0 0.0 copy-done
  4.0 0.0 copy-done.1
  4.0 1.7 %shard_map.50 = (f32[16,3,4,128]{3,2,1,0:T(4,128)S(1)}, f32[192,128]{1,0:T(8,128)S(1)}) custom-call(bf16[128,64,128]{2,1,0:T(8,128)(2,1)S(1)} %bitcast.8, bf16[128,1408]{1,0:T(8,128)(2,1)S(1)} %copy-done, f32[64,384]{1,0:T(8,128)S(1)} %copy-done.1), custom_call_target="tpu_custom_call" | custom-call | tf_op jit(solution)/shard_map/pallas_call | solution.py:149
  5.8 16.1 %all_to_all.35 = f32[16,3,4,128]{3,2,1,0:T(4,128)S(1)} all-to-all(f32[16,3,4,128]{3,2,1,0:T(4,128)S(1)} %get-tuple-element.15), channel_id=1, replica_groups=mesh['zh'=4,'x'=4,'c'=2,'zl'=4,'y'=4] {'y','zl'}, dimensions={0} | all-to-all | bytes 196608 | tf_op jit(solution)/shard_map/all_to_all | solution.py:175
  21.9 9.8 %all_to_all.36.strains_ref = f32[16,3,4,128]{3,2,1,0:T(4,128)S(1)} all-to-all(f32[16,3,4,128]{3,2,1,0:T(4,128)S(1)} %broadcast_in_dim.10), channel_id=1, replica_groups=mesh['zh'=4,'x'=4,'c'=2,'zl'=4,'y'=4] {'y','zl'}, dimensions={0} | all-to-all | bytes 196608 | tf_op jit(solution)/shard_map/all_to_all | solution.py:178
  31.8 1.4 shard_map.51
  33.2 18.8 %all_to_all.37 = f32[8,176,128]{2,1,0:T(8,128)S(1)} all-to-all(f32[8,176,128]{2,1,0:T(8,128)S(1)} %bitcast.14), channel_id=1, replica_groups=mesh['zh'=4,'x'=4,'c'=2,'zl'=4,'y'=4] {'c','x'}, dimensions={0} | all-to-all | bytes 1441792 | tf_op jit(solution)/shard_map/all_to_all | solution.py:175
  52.0 9.8 %collective-permute-start = (f32[176,128]{1,0:T(8,128)S(1)}, f32[176,128]{1,0:T(8,128)S(1)}, u32[]{:S(2)}, u32[]{:S(2)}) collective-permute-start(f32[176,128]{1,0:T(8,128)S(1)} %reduce_sum.48), channel_id=1, source_target_pairs={{0,128},{256,384},{144,272},{400,16},{128,0},{384,256},{272,144},{... | collective-permute-start | bytes 270344 | tf_op jit(solution)/shard_map/ppermute | solution.py:181
  61.8 4.1 %collective-permute-done = f32[176,128]{1,0:T(8,128)S(1)} collective-permute-done((f32[176,128]{1,0:T(8,128)S(1)}, f32[176,128]{1,0:T(8,128)S(1)}, u32[]{:S(2)}, u32[]{:S(2)}) %collective-permute-start) | collective-permute-done | bytes 90144 | tf_op jit(solution)/shard_map/ppermute | solution.py:181
  65.9 7.1 %collective-permute-start.1 = (f32[176,128]{1,0:T(8,128)S(1)}, f32[176,128]{1,0:T(8,128)S(1)}, u32[]{:S(2)}, u32[]{:S(2)}) collective-permute-start(f32[176,128]{1,0:T(8,128)S(1)} %add.6), channel_id=1, source_target_pairs={{128,256},{384,0},{16,144},{272,400},{256,128},{0,384},{144,16},{4... | collective-permute-start | bytes 270344 | tf_op jit(solution)/shard_map/ppermute | solution.py:181
  73.0 3.6 %collective-permute-done.1 = f32[176,128]{1,0:T(8,128)S(1)} collective-permute-done((f32[176,128]{1,0:T(8,128)S(1)}, f32[176,128]{1,0:T(8,128)S(1)}, u32[]{:S(2)}, u32[]{:S(2)}) %collective-permute-start.1) | collective-permute-done | bytes 90144 | tf_op jit(solution)/shard_map/ppermute | solution.py:181
  76.6 8.4 %all_to_all.38 = f32[4,176,128]{2,1,0:T(8,128)S(1)} all-to-all(f32[4,176,128]{2,1,0:T(8,128)S(1)} %broadcast_in_dim.11), channel_id=1, replica_groups=mesh['zh'=4,'x'=4,'c'=2,'zl'=4,'y'=4] {'x'}, dimensions={0} | all-to-all | bytes 720896 | tf_op jit(solution)/shard_map/all_to_all | solution.py:178
  85.0 5.5 %collective-permute-start.2 = (f32[704,128]{1,0:T(8,128)S(1)}, f32[704,128]{1,0:T(8,128)S(1)}, u32[]{:S(2)}, u32[]{:S(2)}) collective-permute-start(f32[704,128]{1,0:T(8,128)S(1)} %bitcast.11), channel_id=1, source_target_pairs={{0,16},{16,0},{1,17},{17,1},{2,18},{18,2},{3,19},{19,3},{4,20},{20... | collective-permute-start | bytes 1081352 | tf_op jit(solution)/shard_map/ppermute | solution.py:181
  90.5 1.3 collective-permute-done.2.other_ref
  91.8 1.7 %shard_map.52 = (f32[16,3,4,128]{3,2,1,0:T(4,128)S(1)}, f32[1,128]{1,0:T(1,128)S(1)}) custom-call(s32[1]{0:T(128)} %bitcast.1.core_ref, bf16[128,64,128]{2,1,0:T(8,128)(2,1)S(1)} %bitcast.10, f32[704,128]{1,0:T(8,128)S(1)} %bitcast.12, f32[704,128]{1,0:T(8,128)S(1)} %collective-permute-done.2.other_ref), custom_call_target="tpu_custom_call" | custom-call | tf_op jit(solution)/shard_map/pallas_call | solution.py:149
  93.5 10.4 %all_to_all.39 = f32[16,3,4,128]{3,2,1,0:T(4,128)S(1)} all-to-all(f32[16,3,4,128]{3,2,1,0:T(4,128)S(1)} %get-tuple-element.18), channel_id=1, replica_groups=mesh['zh'=4,'x'=4,'c'=2,'zl'=4,'y'=4] {'y','zl'}, dimensions={0} | all-to-all | bytes 196608 | tf_op jit(solution)/shard_map/all_to_all | solution.py:175
  104.0 26.1 %all_to_all.40 = f32[32,1,128]{2,1,0:T(1,128)S(1)} all-to-all(f32[32,1,128]{2,1,0:T(1,128)S(1)} %broadcast_in_dim.12), channel_id=1, replica_groups=mesh['zh'=4,'x'=4,'c'=2,'zl'=4,'y'=4] {'zh','x','c'}, dimensions={0} | all-to-all | bytes 32768 | tf_op jit(solution)/shard_map/all_to_all | solution.py:178
  130.1 9.8 %all_to_all.41.image_ref = f32[16,4,4,128]{3,2,1,0:T(4,128)S(1)} all-to-all(f32[16,4,4,128]{3,2,1,0:T(4,128)S(1)} %broadcast_in_dim.14), channel_id=1, replica_groups=mesh['zh'=4,'x'=4,'c'=2,'zl'=4,'y'=4] {'y','zl'}, dimensions={0} | all-to-all | bytes 262144 | tf_op jit(solution)/shard_map/all_to_all | solution.py:178
  139.9 1.4 %shard_map.53 = (f32[128,1408]{1,0:T(8,128)}, f32[64,384]{1,0:T(8,128)}) custom-call(s32[1]{0:T(128)} %bitcast.1.core_ref, bf16[128,1408]{1,0:T(8,128)(2,1)S(1)} %copy-done, f32[704,128]{1,0:T(8,128)S(1)} %bitcast.13, f32[704,128]{1,0:T(8,128)S(1)} %collective-permute-done.2.other_ref, f32[16,4,4,128]{3,2,1,0:T(4,128)S(1)} %all_to_all.41.image_ref, ...), custom_call_target="tpu_custom_call" | custom-call | tf_op jit(solution)/shard_map/pallas_call | solution.py:149
  (13 shorter events, 0.3 us)
Async XLA Ops:
  0.6 3.4 %copy-start = (bf16[128,1408]{1,0:T(8,128)(2,1)S(1)}, bf16[128,1408]{1,0:T(8,128)(2,1)}, u32[]{:S(2)}) copy-start(bf16[128,1408]{1,0:T(8,128)(2,1)} %forces_ref.3) | copy-start | bytes 1081348
  0.6 3.4 %copy-start.1 = (f32[64,384]{1,0:T(8,128)S(1)}, f32[64,384]{1,0:T(8,128)}, u32[]{:S(2)}) copy-start(f32[64,384]{1,0:T(8,128)} %measured_ref.1) | copy-start | bytes 294916
  52.0 13.8 %collective-permute-start = (f32[176,128]{1,0:T(8,128)S(1)}, f32[176,128]{1,0:T(8,128)S(1)}, u32[]{:S(2)}, u32[]{:S(2)}) collective-permute-start(f32[176,128]{1,0:T(8,128)S(1)} %reduce_sum.48), channel_id=1, source_target_pairs={{0,128},{256,384},{144,272},{400,16},{128,0},{384,256},{272,144},{... | collective-permute-start | bytes 270344 | tf_op jit(solution)/shard_map/ppermute | solution.py:181
  65.9 10.6 %collective-permute-start.1 = (f32[176,128]{1,0:T(8,128)S(1)}, f32[176,128]{1,0:T(8,128)S(1)}, u32[]{:S(2)}, u32[]{:S(2)}) collective-permute-start(f32[176,128]{1,0:T(8,128)S(1)} %add.6), channel_id=1, source_target_pairs={{128,256},{384,0},{16,144},{272,400},{256,128},{0,384},{144,16},{4... | collective-permute-start | bytes 270344 | tf_op jit(solution)/shard_map/ppermute | solution.py:181
  85.0 6.8 %collective-permute-start.2 = (f32[704,128]{1,0:T(8,128)S(1)}, f32[704,128]{1,0:T(8,128)S(1)}, u32[]{:S(2)}, u32[]{:S(2)}) collective-permute-start(f32[704,128]{1,0:T(8,128)S(1)} %bitcast.11), channel_id=1, source_target_pairs={{0,16},{16,0},{1,17},{17,1},{2,18},{18,2},{3,19},{19,3},{4,20},{20... | collective-permute-start | bytes 1081352 | tf_op jit(solution)/shard_map/ppermute | solution.py:181

commit v6 on v5

--- a/solution.py
+++ b/solution.py
@@ -80,7 +80,7 @@
     measured_t_ref[:, hots:2 * hots] = measured_t[half:]
 
 
-def gradient_kernel(taps_ref, strains_ref, measured_t_ref, part_ref, residual_ref, packed, padded, windows):
+def gradient_kernel(core_ref, taps_ref, strains_ref, measured_t_ref, kept_ref, sent_ref, residual_ref, packed, padded, windows, total):
     hots = taps_ref.shape[1]
     half = SEG_COLS // 2
     unpack_strains(strains_ref, packed)
@@ -107,10 +107,13 @@
                 piece = out[row * LANES:(row + 1) * LANES, side * LANES:(side + 1) * LANES]
                 cols = slice(block * LANES, (block + 1) * LANES)
                 if block in seen:
-                    part_ref[cols, :] += piece
+                    total[cols, :] += piece
                 else:
-                    part_ref[cols, :] = piece
+                    total[cols, :] = piece
                     seen.add(block)
+    rows = kept_ref.shape[0]
+    kept_ref[...] = total[pl.ds(pl.multiple_of(core_ref[0] * rows, rows), rows), :]
+    sent_ref[...] = total[pl.ds(pl.multiple_of((1 - core_ref[0]) * rows, rows), rows), :]
 
 
 def join_halves(core_ref, own_ref, other_ref, signal_t):
@@ -163,6 +166,7 @@
     half = SEG_COLS // 2
     part = jax.ShapeDtypeStruct((peers, half // peers // GROUP, GROUP, LANES), F32)
     packed_shape = jax.ShapeDtypeStruct((half, 2 * hots), F32)
+    core_shape = jax.ShapeDtypeStruct((COLS // 2, loads), F32)
     forward_scratch = [
         pltpu.VMEM((COLS, loads), F32),
         pltpu.VMEM((half, 2 * hots), F32),
@@ -185,19 +189,20 @@
         strain_kernel, (part, packed_shape), forward_scratch, (taps, forces, measured)
     )
     strains = gather(scatter_sum(strain_part, load_axes), load_axes)
-    gradient_part, residual = call(
+    kept, sent, residual = call(
         gradient_kernel,
-        (jax.ShapeDtypeStruct((COLS, loads), F32), packed_shape),
+        (core_shape, core_shape, packed_shape),
         [
             pltpu.VMEM((half, 2 * hots), F32),
             pltpu.VMEM((SEG_COLS + 2 * LANES, 2 * hots), F32),
             pltpu.VMEM((SEG_COLS + LANES, PHASES * hots), BF16),
+            pltpu.VMEM((COLS, loads), F32),
         ],
-        (taps, strains, measured_t),
+        (core, taps, strains, measured_t),
     )
     cores = [(0, 1)]
-    near = ("c", "x")
-    own = scatter_sum(gradient_part.reshape(lax.axis_size(near), -1, loads), near)
+    own = kept + swapped(sent, "c", cores)
+    own = scatter_sum(own.reshape(lax.axis_size("x"), -1, loads), "x")
     inner, outer = [(0, 1), (2, 3)], [(1, 2), (3, 0)]
     for even, odd in ((inner, outer), (outer, inner)):
         pairs = [(2 * i, 2 * j) for i, j in even] + [(2 * i + 1, 2 * j + 1) for i, j in odd]

time: 142 us -> 141 us (level)
  blocking collectives: 99.5 us -> 90.3 us
  starting transfers between devices: 22.3 us -> 28.4 us
  waiting for transfers between devices: 8.89 us -> 10.7 us
    all_to_all x3, blocking collectives: 45.4 us -> 36.5 us  [scatter_sum(): return jnp.sum(lax.all_to_all(value, axis, 0, 0), axis=0)]
    ppermute x3 -> x4, starting transfers between devices: 22.3 us -> 28.4 us  [swapped(): return lax.ppermute(value, axis, pairs + [(b, a) for a, b in pairs])]
    ppermute x3 -> x4, waiting for transfers between devices: 8.89 us -> 10.7 us  [swapped(): return lax.ppermute(value, axis, pairs + [(b, a) for a, b in pairs])]
  transfers between devices with their start and end apart: 3 -> 4, of which waited for: 3 -> 4; matrix products, arithmetic and copies ran while one was open for 0% -> 0% of each run, Pallas kernels for 0% -> 0%
where the time goes in v6:
time: 141 us; the launch traced here: 140 us
  blocking collectives  90.3 us (64%)
  starting transfers between devices  28.4 us (20%)
  waiting for transfers between devices  10.7 us (8%)
  Pallas kernels  6.33 us (4%)
  local copies, waits for them, and re-layouts  3.43 us (2%)
    all_to_all x4, blocking collectives, gather(): return lax.all_to_all(spread(value, lax.axis_size(axis)), axis, 0, 0)  53.7 us
    all_to_all x3, blocking collectives, scatter_sum(): return jnp.sum(lax.all_to_all(value, axis, 0, 0), axis=0)  36.5 us
    ppermute x4, starting transfers between devices, swapped(): return lax.ppermute(value, axis, pairs + [(b, a) for a, b in pairs])  28.4 us
    ppermute x4, waiting for transfers between devices, swapped(): return lax.ppermute(value, axis, pairs + [(b, a) for a, b in pairs])  10.7 us
    pallas_call x4, Pallas kernels, call(): pl.pallas_call(kernel, out_shape=outs, in_specs=[pl.BlockSpec(memory_spac...  6.33 us
    unnamed x5, local copies, waits for them, and re-layouts  3.36 us
  transfers between devices with their start and end apart: 4, of which 4 were waited for; matrix products, arithmetic and copies ran while one was open for 0% of the time, Pallas kernels for 0%

profile of v6, /device:TPU:1, one launch (start us, length us, event | category | flops | bytes accessed | tf_op | source)
XLA Modules:
  0.0 140.2 jit_solution(12845038900441454525)
XLA Ops:
  0.6 0.0 copy-start
  0.6 0.0 copy-start.1
  0.7 3.3 %copy.7 = bf16[64,128,128]{1,0,2:T(8,128)(2,1)S(1)} copy(bf16[64,128,128]{2,1,0:T(8,128)(2,1)} %param.3) | data formatting | bytes 4194304 | tf_op args[0]
  4.0 0.0 copy-done
  4.0 0.0 copy-done.1
  4.0 1.7 %shard_map.50 = (f32[16,3,4,128]{3,2,1,0:T(4,128)S(1)}, f32[192,128]{1,0:T(8,128)S(1)}) custom-call(bf16[128,64,128]{2,1,0:T(8,128)(2,1)S(1)} %bitcast.8, bf16[128,1408]{1,0:T(8,128)(2,1)S(1)} %copy-done, f32[64,384]{1,0:T(8,128)S(1)} %copy-done.1), custom_call_target="tpu_custom_call" | custom-call | tf_op jit(solution)/shard_map/pallas_call | solution.py:152
  5.8 16.1 %all_to_all.35 = f32[16,3,4,128]{3,2,1,0:T(4,128)S(1)} all-to-all(f32[16,3,4,128]{3,2,1,0:T(4,128)S(1)} %get-tuple-element.16), channel_id=1, replica_groups=mesh['zh'=4,'x'=4,'c'=2,'zl'=4,'y'=4] {'y','zl'}, dimensions={0} | all-to-all | bytes 196608 | tf_op jit(solution)/shard_map/all_to_all | solution.py:179
  21.9 9.8 %all_to_all.36.strains_ref = f32[16,3,4,128]{3,2,1,0:T(4,128)S(1)} all-to-all(f32[16,3,4,128]{3,2,1,0:T(4,128)S(1)} %broadcast_in_dim.10), channel_id=1, replica_groups=mesh['zh'=4,'x'=4,'c'=2,'zl'=4,'y'=4] {'y','zl'}, dimensions={0} | all-to-all | bytes 196608 | tf_op jit(solution)/shard_map/all_to_all | solution.py:182
  31.8 1.4 %shard_map.51 = (f32[704,128]{1,0:T(8,128)S(1)}, f32[704,128]{1,0:T(8,128)S(1)}, f32[192,128]{1,0:T(8,128)S(1)}) custom-call(s32[1]{0:T(128)} %bitcast.1.core_ref, bf16[128,64,128]{2,1,0:T(8,128)(2,1)S(1)} %bitcast.9, f32[16,3,4,128]{3,2,1,0:T(4,128)S(1)} %all_to_all.36.strains_ref, f32[192,128]{1,0:T(8,128)S(1)} %get-tuple-element.17.measured_t_ref), custom_call_target="tpu_custom_call" | custom-call | tf_op jit(solution)/shard_map/pallas_call | solution.py:152
  33.2 5.1 %collective-permute-start = (f32[704,128]{1,0:T(8,128)S(1)}, f32[704,128]{1,0:T(8,128)S(1)}, u32[]{:S(2)}, u32[]{:S(2)}) collective-permute-start(f32[704,128]{1,0:T(8,128)S(1)} %get-tuple-element.19), channel_id=1, source_target_pairs={{0,16},{16,0},{1,17},{17,1},{2,18},{18,2},{3,19},{19,3},{4,20},{20... | collective-permute-start | bytes 1081352 | tf_op jit(solution)/shard_map/ppermute | solution.py:185
  38.4 1.3 collective-permute-done
  39.6 0.1 add.9
  39.7 10.8 %all_to_all.37 = f32[4,176,128]{2,1,0:T(8,128)S(1)} all-to-all(f32[4,176,128]{2,1,0:T(8,128)S(1)} %bitcast.14), channel_id=1, replica_groups=mesh['zh'=4,'x'=4,'c'=2,'zl'=4,'y'=4] {'x'}, dimensions={0} | all-to-all | bytes 720896 | tf_op jit(solution)/shard_map/all_to_all | solution.py:179
  50.5 9.8 %collective-permute-start.1 = (f32[176,128]{1,0:T(8,128)S(1)}, f32[176,128]{1,0:T(8,128)S(1)}, u32[]{:S(2)}, u32[]{:S(2)}) collective-permute-start(f32[176,128]{1,0:T(8,128)S(1)} %reduce_sum.48), channel_id=1, source_target_pairs={{0,128},{256,384},{144,272},{400,16},{128,0},{384,256},{272,144},{... | collective-permute-start | bytes 270344 | tf_op jit(solution)/shard_map/ppermute | solution.py:185
  60.3 4.3 %collective-permute-done.1 = f32[176,128]{1,0:T(8,128)S(1)} collective-permute-done((f32[176,128]{1,0:T(8,128)S(1)}, f32[176,128]{1,0:T(8,128)S(1)}, u32[]{:S(2)}, u32[]{:S(2)}) %collective-permute-start.1) | collective-permute-done | bytes 90144 | tf_op jit(solution)/shard_map/ppermute | solution.py:185
  64.6 6.8 %collective-permute-start.2 = (f32[176,128]{1,0:T(8,128)S(1)}, f32[176,128]{1,0:T(8,128)S(1)}, u32[]{:S(2)}, u32[]{:S(2)}) collective-permute-start(f32[176,128]{1,0:T(8,128)S(1)} %add.10), channel_id=1, source_target_pairs={{128,256},{384,0},{16,144},{272,400},{256,128},{0,384},{144,16},{4... | collective-permute-start | bytes 270344 | tf_op jit(solution)/shard_map/ppermute | solution.py:185
  71.4 3.8 %collective-permute-done.2 = f32[176,128]{1,0:T(8,128)S(1)} collective-permute-done((f32[176,128]{1,0:T(8,128)S(1)}, f32[176,128]{1,0:T(8,128)S(1)}, u32[]{:S(2)}, u32[]{:S(2)}) %collective-permute-start.2) | collective-permute-done | bytes 90144 | tf_op jit(solution)/shard_map/ppermute | solution.py:185
  75.3 8.4 %all_to_all.38 = f32[4,176,128]{2,1,0:T(8,128)S(1)} all-to-all(f32[4,176,128]{2,1,0:T(8,128)S(1)} %broadcast_in_dim.11), channel_id=1, replica_groups=mesh['zh'=4,'x'=4,'c'=2,'zl'=4,'y'=4] {'x'}, dimensions={0} | all-to-all | bytes 720896 | tf_op jit(solution)/shard_map/all_to_all | solution.py:182
  83.7 6.7 %collective-permute-start.3 = (f32[704,128]{1,0:T(8,128)S(1)}, f32[704,128]{1,0:T(8,128)S(1)}, u32[]{:S(2)}, u32[]{:S(2)}) collective-permute-start(f32[704,128]{1,0:T(8,128)S(1)} %bitcast.11), channel_id=1, source_target_pairs={{0,16},{16,0},{1,17},{17,1},{2,18},{18,2},{3,19},{19,3},{4,20},{20... | collective-permute-start | bytes 1081352 | tf_op jit(solution)/shard_map/ppermute | solution.py:185
  90.4 1.3 collective-permute-done.3.other_ref
  91.7 1.7 %shard_map.52 = (f32[16,3,4,128]{3,2,1,0:T(4,128)S(1)}, f32[1,128]{1,0:T(1,128)S(1)}) custom-call(s32[1]{0:T(128)} %bitcast.1.core_ref, bf16[128,64,128]{2,1,0:T(8,128)(2,1)S(1)} %bitcast.10, f32[704,128]{1,0:T(8,128)S(1)} %bitcast.12, f32[704,128]{1,0:T(8,128)S(1)} %collective-permute-done.3.other_ref), custom_call_target="tpu_custom_call" | custom-call | tf_op jit(solution)/shard_map/pallas_call | solution.py:152
  93.4 9.7 %all_to_all.39 = f32[16,3,4,128]{3,2,1,0:T(4,128)S(1)} all-to-all(f32[16,3,4,128]{3,2,1,0:T(4,128)S(1)} %get-tuple-element.20), channel_id=1, replica_groups=mesh['zh'=4,'x'=4,'c'=2,'zl'=4,'y'=4] {'y','zl'}, dimensions={0} | all-to-all | bytes 196608 | tf_op jit(solution)/shard_map/all_to_all | solution.py:179
  103.2 25.7 %all_to_all.40 = f32[32,1,128]{2,1,0:T(1,128)S(1)} all-to-all(f32[32,1,128]{2,1,0:T(1,128)S(1)} %broadcast_in_dim.12), channel_id=1, replica_groups=mesh['zh'=4,'x'=4,'c'=2,'zl'=4,'y'=4] {'zh','x','c'}, dimensions={0} | all-to-all | bytes 32768 | tf_op jit(solution)/shard_map/all_to_all | solution.py:182
  128.9 9.8 %all_to_all.41.image_ref = f32[16,4,4,128]{3,2,1,0:T(4,128)S(1)} all-to-all(f32[16,4,4,128]{3,2,1,0:T(4,128)S(1)} %broadcast_in_dim.14), channel_id=1, replica_groups=mesh['zh'=4,'x'=4,'c'=2,'zl'=4,'y'=4] {'y','zl'}, dimensions={0} | all-to-all | bytes 262144 | tf_op jit(solution)/shard_map/all_to_all | solution.py:182
  138.7 1.4 %shard_map.53 = (f32[128,1408]{1,0:T(8,128)}, f32[64,384]{1,0:T(8,128)}) custom-call(s32[1]{0:T(128)} %bitcast.1.core_ref, bf16[128,1408]{1,0:T(8,128)(2,1)S(1)} %copy-done, f32[704,128]{1,0:T(8,128)S(1)} %bitcast.13, f32[704,128]{1,0:T(8,128)S(1)} %collective-permute-done.3.other_ref, f32[16,4,4,128]{3,2,1,0:T(4,128)S(1)} %all_to_all.41.image_ref, ...), custom_call_target="tpu_custom_call" | custom-call | tf_op jit(solution)/shard_map/pallas_call | solution.py:152
  (13 shorter events, 0.3 us)
Async XLA Ops:
  0.6 3.4 %copy-start = (bf16[128,1408]{1,0:T(8,128)(2,1)S(1)}, bf16[128,1408]{1,0:T(8,128)(2,1)}, u32[]{:S(2)}) copy-start(bf16[128,1408]{1,0:T(8,128)(2,1)} %forces_ref.3) | copy-start | bytes 1081348
  0.6 3.4 %copy-start.1 = (f32[64,384]{1,0:T(8,128)S(1)}, f32[64,384]{1,0:T(8,128)}, u32[]{:S(2)}) copy-start(f32[64,384]{1,0:T(8,128)} %measured_ref.1) | copy-start | bytes 294916
  33.2 6.4 %collective-permute-start = (f32[704,128]{1,0:T(8,128)S(1)}, f32[704,128]{1,0:T(8,128)S(1)}, u32[]{:S(2)}, u32[]{:S(2)}) collective-permute-start(f32[704,128]{1,0:T(8,128)S(1)} %get-tuple-element.19), channel_id=1, source_target_pairs={{0,16},{16,0},{1,17},{17,1},{2,18},{18,2},{3,19},{19,3},{4,20},{20... | collective-permute-start | bytes 1081352 | tf_op jit(solution)/shard_map/ppermute | solution.py:185
  50.5 14.1 %collective-permute-start.1 = (f32[176,128]{1,0:T(8,128)S(1)}, f32[176,128]{1,0:T(8,128)S(1)}, u32[]{:S(2)}, u32[]{:S(2)}) collective-permute-start(f32[176,128]{1,0:T(8,128)S(1)} %reduce_sum.48), channel_id=1, source_target_pairs={{0,128},{256,384},{144,272},{400,16},{128,0},{384,256},{272,144},{... | collective-permute-start | bytes 270344 | tf_op jit(solution)/shard_map/ppermute | solution.py:185
  64.6 10.6 %collective-permute-start.2 = (f32[176,128]{1,0:T(8,128)S(1)}, f32[176,128]{1,0:T(8,128)S(1)}, u32[]{:S(2)}, u32[]{:S(2)}) collective-permute-start(f32[176,128]{1,0:T(8,128)S(1)} %add.10), channel_id=1, source_target_pairs={{128,256},{384,0},{16,144},{272,400},{256,128},{0,384},{144,16},{4... | collective-permute-start | bytes 270344 | tf_op jit(solution)/shard_map/ppermute | solution.py:185
  83.7 8.0 %collective-permute-start.3 = (f32[704,128]{1,0:T(8,128)S(1)}, f32[704,128]{1,0:T(8,128)S(1)}, u32[]{:S(2)}, u32[]{:S(2)}) collective-permute-start(f32[704,128]{1,0:T(8,128)S(1)} %bitcast.11), channel_id=1, source_target_pairs={{0,16},{16,0},{1,17},{17,1},{2,18},{18,2},{3,19},{19,3},{4,20},{20... | collective-permute-start | bytes 1081352 | tf_op jit(solution)/shard_map/ppermute | solution.py:185

commit v7 on v6

--- a/solution.py
+++ b/solution.py
@@ -214,7 +214,7 @@
     )
     image = scatter_sum(image_part, load_axes)
     squares = jnp.sum(image * image, axis=(0, 1))[None]
-    squares = jnp.sum(gather(squares, ("zh", "x", "c")), axis=0)
+    squares = jnp.sum(gather(squares, ("x", "zh", "c")), axis=0)
     image, squares, own_squares = lax.optimization_barrier((image, squares, own_squares))
     extra = jnp.concatenate([squares, own_squares] * (GROUP // 2), axis=0)
     image = gather(jnp.concatenate([image, extra[None]], axis=0), load_axes)

time: 141 us -> 141 us (level)
  no operation moved by 1% of the time
where the time goes in v7:
time: 141 us; the launch traced here: 140 us
  blocking collectives  90.3 us (64%)
  starting transfers between devices  28.4 us (20%)
  waiting for transfers between devices  10.7 us (8%)
  Pallas kernels  6.33 us (4%)
  local copies, waits for them, and re-layouts  3.43 us (2%)
    all_to_all x4, blocking collectives, gather(): return lax.all_to_all(spread(value, lax.axis_size(axis)), axis, 0, 0)  53.7 us
    all_to_all x3, blocking collectives, scatter_sum(): return jnp.sum(lax.all_to_all(value, axis, 0, 0), axis=0)  36.5 us
    ppermute x4, starting transfers between devices, swapped(): return lax.ppermute(value, axis, pairs + [(b, a) for a, b in pairs])  28.4 us
    ppermute x4, waiting for transfers between devices, swapped(): return lax.ppermute(value, axis, pairs + [(b, a) for a, b in pairs])  10.7 us
    pallas_call x4, Pallas kernels, call(): pl.pallas_call(kernel, out_shape=outs, in_specs=[pl.BlockSpec(memory_spac...  6.33 us
    unnamed x5, local copies, waits for them, and re-layouts  3.36 us
  transfers between devices with their start and end apart: 4, of which 4 were waited for; matrix products, arithmetic and copies ran while one was open for 0% of the time, Pallas kernels for 0%

profile of v7, /device:TPU:1, one launch (start us, length us, event | category | flops | bytes accessed | tf_op | source)
XLA Modules:
  0.0 140.2 jit_solution(17564593048821830240)
XLA Ops:
  0.6 0.0 copy-start
  0.6 0.0 copy-start.1
  0.7 3.3 %copy.7 = bf16[64,128,128]{1,0,2:T(8,128)(2,1)S(1)} copy(bf16[64,128,128]{2,1,0:T(8,128)(2,1)} %param.3) | data formatting | bytes 4194304 | tf_op args[0]
  4.0 0.0 copy-done
  4.0 0.0 copy-done.1
  4.0 1.7 %shard_map.50 = (f32[16,3,4,128]{3,2,1,0:T(4,128)S(1)}, f32[192,128]{1,0:T(8,128)S(1)}) custom-call(bf16[128,64,128]{2,1,0:T(8,128)(2,1)S(1)} %bitcast.8, bf16[128,1408]{1,0:T(8,128)(2,1)S(1)} %copy-done, f32[64,384]{1,0:T(8,128)S(1)} %copy-done.1), custom_call_target="tpu_custom_call" | custom-call | tf_op jit(solution)/shard_map/pallas_call | solution.py:152
  5.8 16.1 %all_to_all.35 = f32[16,3,4,128]{3,2,1,0:T(4,128)S(1)} all-to-all(f32[16,3,4,128]{3,2,1,0:T(4,128)S(1)} %get-tuple-element.16), channel_id=1, replica_groups=mesh['zh'=4,'x'=4,'c'=2,'zl'=4,'y'=4] {'y','zl'}, dimensions={0} | all-to-all | bytes 196608 | tf_op jit(solution)/shard_map/all_to_all | solution.py:179
  21.9 9.8 %all_to_all.36.strains_ref = f32[16,3,4,128]{3,2,1,0:T(4,128)S(1)} all-to-all(f32[16,3,4,128]{3,2,1,0:T(4,128)S(1)} %broadcast_in_dim.10), channel_id=1, replica_groups=mesh['zh'=4,'x'=4,'c'=2,'zl'=4,'y'=4] {'y','zl'}, dimensions={0} | all-to-all | bytes 196608 | tf_op jit(solution)/shard_map/all_to_all | solution.py:182
  31.8 1.4 %shard_map.51 = (f32[704,128]{1,0:T(8,128)S(1)}, f32[704,128]{1,0:T(8,128)S(1)}, f32[192,128]{1,0:T(8,128)S(1)}) custom-call(s32[1]{0:T(128)} %bitcast.1.core_ref, bf16[128,64,128]{2,1,0:T(8,128)(2,1)S(1)} %bitcast.9, f32[16,3,4,128]{3,2,1,0:T(4,128)S(1)} %all_to_all.36.strains_ref, f32[192,128]{1,0:T(8,128)S(1)} %get-tuple-element.17.measured_t_ref), custom_call_target="tpu_custom_call" | custom-call | tf_op jit(solution)/shard_map/pallas_call | solution.py:152
  33.2 5.1 %collective-permute-start = (f32[704,128]{1,0:T(8,128)S(1)}, f32[704,128]{1,0:T(8,128)S(1)}, u32[]{:S(2)}, u32[]{:S(2)}) collective-permute-start(f32[704,128]{1,0:T(8,128)S(1)} %get-tuple-element.19), channel_id=1, source_target_pairs={{0,16},{16,0},{1,17},{17,1},{2,18},{18,2},{3,19},{19,3},{4,20},{20... | collective-permute-start | bytes 1081352 | tf_op jit(solution)/shard_map/ppermute | solution.py:185
  38.4 1.3 collective-permute-done
  39.6 0.1 add.9
  39.7 10.8 %all_to_all.37 = f32[4,176,128]{2,1,0:T(8,128)S(1)} all-to-all(f32[4,176,128]{2,1,0:T(8,128)S(1)} %bitcast.14), channel_id=1, replica_groups=mesh['zh'=4,'x'=4,'c'=2,'zl'=4,'y'=4] {'x'}, dimensions={0} | all-to-all | bytes 720896 | tf_op jit(solution)/shard_map/all_to_all | solution.py:179
  50.5 9.8 %collective-permute-start.1 = (f32[176,128]{1,0:T(8,128)S(1)}, f32[176,128]{1,0:T(8,128)S(1)}, u32[]{:S(2)}, u32[]{:S(2)}) collective-permute-start(f32[176,128]{1,0:T(8,128)S(1)} %reduce_sum.48), channel_id=1, source_target_pairs={{0,128},{256,384},{144,272},{400,16},{128,0},{384,256},{272,144},{... | collective-permute-start | bytes 270344 | tf_op jit(solution)/shard_map/ppermute | solution.py:185
  60.3 4.3 %collective-permute-done.1 = f32[176,128]{1,0:T(8,128)S(1)} collective-permute-done((f32[176,128]{1,0:T(8,128)S(1)}, f32[176,128]{1,0:T(8,128)S(1)}, u32[]{:S(2)}, u32[]{:S(2)}) %collective-permute-start.1) | collective-permute-done | bytes 90144 | tf_op jit(solution)/shard_map/ppermute | solution.py:185
  64.6 6.8 %collective-permute-start.2 = (f32[176,128]{1,0:T(8,128)S(1)}, f32[176,128]{1,0:T(8,128)S(1)}, u32[]{:S(2)}, u32[]{:S(2)}) collective-permute-start(f32[176,128]{1,0:T(8,128)S(1)} %add.10), channel_id=1, source_target_pairs={{128,256},{384,0},{16,144},{272,400},{256,128},{0,384},{144,16},{4... | collective-permute-start | bytes 270344 | tf_op jit(solution)/shard_map/ppermute | solution.py:185
  71.4 3.8 %collective-permute-done.2 = f32[176,128]{1,0:T(8,128)S(1)} collective-permute-done((f32[176,128]{1,0:T(8,128)S(1)}, f32[176,128]{1,0:T(8,128)S(1)}, u32[]{:S(2)}, u32[]{:S(2)}) %collective-permute-start.2) | collective-permute-done | bytes 90144 | tf_op jit(solution)/shard_map/ppermute | solution.py:185
  75.3 8.4 %all_to_all.38 = f32[4,176,128]{2,1,0:T(8,128)S(1)} all-to-all(f32[4,176,128]{2,1,0:T(8,128)S(1)} %broadcast_in_dim.11), channel_id=1, replica_groups=mesh['zh'=4,'x'=4,'c'=2,'zl'=4,'y'=4] {'x'}, dimensions={0} | all-to-all | bytes 720896 | tf_op jit(solution)/shard_map/all_to_all | solution.py:182
  83.7 6.7 %collective-permute-start.3 = (f32[704,128]{1,0:T(8,128)S(1)}, f32[704,128]{1,0:T(8,128)S(1)}, u32[]{:S(2)}, u32[]{:S(2)}) collective-permute-start(f32[704,128]{1,0:T(8,128)S(1)} %bitcast.11), channel_id=1, source_target_pairs={{0,16},{16,0},{1,17},{17,1},{2,18},{18,2},{3,19},{19,3},{4,20},{20... | collective-permute-start | bytes 1081352 | tf_op jit(solution)/shard_map/ppermute | solution.py:185
  90.4 1.3 collective-permute-done.3.other_ref
  91.7 1.7 %shard_map.52 = (f32[16,3,4,128]{3,2,1,0:T(4,128)S(1)}, f32[1,128]{1,0:T(1,128)S(1)}) custom-call(s32[1]{0:T(128)} %bitcast.1.core_ref, bf16[128,64,128]{2,1,0:T(8,128)(2,1)S(1)} %bitcast.10, f32[704,128]{1,0:T(8,128)S(1)} %bitcast.12, f32[704,128]{1,0:T(8,128)S(1)} %collective-permute-done.3.other_ref), custom_call_target="tpu_custom_call" | custom-call | tf_op jit(solution)/shard_map/pallas_call | solution.py:152
  93.4 9.7 %all_to_all.39 = f32[16,3,4,128]{3,2,1,0:T(4,128)S(1)} all-to-all(f32[16,3,4,128]{3,2,1,0:T(4,128)S(1)} %get-tuple-element.20), channel_id=1, replica_groups=mesh['zh'=4,'x'=4,'c'=2,'zl'=4,'y'=4] {'y','zl'}, dimensions={0} | all-to-all | bytes 196608 | tf_op jit(solution)/shard_map/all_to_all | solution.py:179
  103.2 25.6 %all_to_all.40 = f32[32,1,128]{2,1,0:T(1,128)S(1)} all-to-all(f32[32,1,128]{2,1,0:T(1,128)S(1)} %broadcast_in_dim.12), channel_id=1, replica_groups=mesh['zh'=4,'x'=4,'c'=2,'zl'=4,'y'=4] {'x','zh','c'}, dimensions={0} | all-to-all | bytes 32768 | tf_op jit(solution)/shard_map/all_to_all | solution.py:182
  128.9 9.9 %all_to_all.41.image_ref = f32[16,4,4,128]{3,2,1,0:T(4,128)S(1)} all-to-all(f32[16,4,4,128]{3,2,1,0:T(4,128)S(1)} %broadcast_in_dim.14), channel_id=1, replica_groups=mesh['zh'=4,'x'=4,'c'=2,'zl'=4,'y'=4] {'y','zl'}, dimensions={0} | all-to-all | bytes 262144 | tf_op jit(solution)/shard_map/all_to_all | solution.py:182
  138.7 1.4 %shard_map.53 = (f32[128,1408]{1,0:T(8,128)}, f32[64,384]{1,0:T(8,128)}) custom-call(s32[1]{0:T(128)} %bitcast.1.core_ref, bf16[128,1408]{1,0:T(8,128)(2,1)S(1)} %copy-done, f32[704,128]{1,0:T(8,128)S(1)} %bitcast.13, f32[704,128]{1,0:T(8,128)S(1)} %collective-permute-done.3.other_ref, f32[16,4,4,128]{3,2,1,0:T(4,128)S(1)} %all_to_all.41.image_ref, ...), custom_call_target="tpu_custom_call" | custom-call | tf_op jit(solution)/shard_map/pallas_call | solution.py:152
  (13 shorter events, 0.3 us)
Async XLA Ops:
  0.6 3.4 %copy-start = (bf16[128,1408]{1,0:T(8,128)(2,1)S(1)}, bf16[128,1408]{1,0:T(8,128)(2,1)}, u32[]{:S(2)}) copy-start(bf16[128,1408]{1,0:T(8,128)(2,1)} %forces_ref.3) | copy-start | bytes 1081348
  0.6 3.4 %copy-start.1 = (f32[64,384]{1,0:T(8,128)S(1)}, f32[64,384]{1,0:T(8,128)}, u32[]{:S(2)}) copy-start(f32[64,384]{1,0:T(8,128)} %measured_ref.1) | copy-start | bytes 294916
  33.2 6.4 %collective-permute-start = (f32[704,128]{1,0:T(8,128)S(1)}, f32[704,128]{1,0:T(8,128)S(1)}, u32[]{:S(2)}, u32[]{:S(2)}) collective-permute-start(f32[704,128]{1,0:T(8,128)S(1)} %get-tuple-element.19), channel_id=1, source_target_pairs={{0,16},{16,0},{1,17},{17,1},{2,18},{18,2},{3,19},{19,3},{4,20},{20... | collective-permute-start | bytes 1081352 | tf_op jit(solution)/shard_map/ppermute | solution.py:185
  50.5 14.1 %collective-permute-start.1 = (f32[176,128]{1,0:T(8,128)S(1)}, f32[176,128]{1,0:T(8,128)S(1)}, u32[]{:S(2)}, u32[]{:S(2)}) collective-permute-start(f32[176,128]{1,0:T(8,128)S(1)} %reduce_sum.48), channel_id=1, source_target_pairs={{0,128},{256,384},{144,272},{400,16},{128,0},{384,256},{272,144},{... | collective-permute-start | bytes 270344 | tf_op jit(solution)/shard_map/ppermute | solution.py:185
  64.6 10.6 %collective-permute-start.2 = (f32[176,128]{1,0:T(8,128)S(1)}, f32[176,128]{1,0:T(8,128)S(1)}, u32[]{:S(2)}, u32[]{:S(2)}) collective-permute-start(f32[176,128]{1,0:T(8,128)S(1)} %add.10), channel_id=1, source_target_pairs={{128,256},{384,0},{16,144},{272,400},{256,128},{0,384},{144,16},{4... | collective-permute-start | bytes 270344 | tf_op jit(solution)/shard_map/ppermute | solution.py:185
  83.7 8.0 %collective-permute-start.3 = (f32[704,128]{1,0:T(8,128)S(1)}, f32[704,128]{1,0:T(8,128)S(1)}, u32[]{:S(2)}, u32[]{:S(2)}) collective-permute-start(f32[704,128]{1,0:T(8,128)S(1)} %bitcast.11), channel_id=1, source_target_pairs={{0,16},{16,0},{1,17},{17,1},{2,18},{18,2},{3,19},{19,3},{4,20},{20... | collective-permute-start | bytes 1081352 | tf_op jit(solution)/shard_map/ppermute | solution.py:185
